TPU v7x, 32 devices: a whole 2x2x4 slice. The times are simulated.
32 devices in a mesh: sub: 32 (over z, y, x, core).
Axes of the slice: x: 2, y: 2, z: 4, core: 2. Of those that a mesh axis runs over, the one named last changes fastest.
Arguments:
- images: float32 [2, 4, 512, 4096], P(None, None, 'sub'), may hold values from -6 to 6
- anchors: int32 [128], P('sub'), may hold values from 0 to 4095, as said below
- patches: int32 [128], P('sub'), may hold values from 0 to 31
- coeffs: float32 [4, 45, 32], P(None, None, 'sub'), may hold values from -1.2 to 1.2
- zbasis: float32 [45, 4096], replicated, may hold values from -4 to 4
Outputs:
- new_coeffs: float32 [4, 45, 32], P(None, None, 'sub')
- last_gradient: float32 [4, 45, 32], P(None, None, 'sub')
Inputs may be any that keep to these rules, and one draw needn't show every extreme that they name: `anchors`: the first column of subfield s lies among the 128 columns that begin at 128 * (s // 4).
All inputs are finite; a program needn't handle non-finite values.
Results may differ from a plain program's by a relative error of at most 0.0003.
Values sent between devices are 32-bit elements; how exact they have to be, the bound alone decides.
A program may use at most 128 MiB of HBM per device.

v0:
```python
import math

import jax
import jax.numpy as jnp
from jax import lax
from jax.sharding import PartitionSpec as P

SUB = 128
CH = 2
TR = 4
ITERS = 2
PUP = 64


GAMMA = 0.01
STEP_SIZE = 0.05


def from_behind(block, axis, distance):
    devices = range(lax.axis_size(axis))
    route = [(i - distance, i) for i in devices if i - distance in devices]
    return lax.ppermute(block, axis, route)


def taper(length):
    cells = jnp.arange(length, dtype=jnp.float32)
    return 0.5 - 0.5 * jnp.cos(2.0 * math.pi * (cells + 0.5) / length)


def aperture(width):
    centred = jnp.arange(width, dtype=jnp.float32) - width / 2 + 0.5
    radius = centred[:, None] ** 2 + centred[None, :] ** 2
    return (radius <= (width / 2) ** 2).astype(jnp.float32)


def dft_tables(length):
    indices = jnp.arange(length, dtype=jnp.int32)
    product_mod = indices[:, None] * indices[None, :] % length
    angles = 2.0 * math.pi / length * product_mod.astype(jnp.float32)
    return (jnp.cos(angles), -jnp.sin(angles))


def complex_dft(real_part, imag_part, left_table, right_table):
    highest = lax.Precision.HIGHEST
    right_real, right_imag = right_table
    left_real, left_imag = left_table
    half_real = jnp.einsum("...ab,kb->...ak", real_part, right_real, precision=highest)
    half_imag = jnp.einsum("...ab,kb->...ak", real_part, right_imag, precision=highest)
    if imag_part is not None:
        half_real = half_real - jnp.einsum(
            "...ab,kb->...ak", imag_part, right_imag, precision=highest
        )
        half_imag = half_imag + jnp.einsum(
            "...ab,kb->...ak", imag_part, right_real, precision=highest
        )
    out_real = jnp.einsum("ja,...ak->...jk", left_real, half_real, precision=highest) - jnp.einsum(
        "ja,...ak->...jk", left_imag, half_imag, precision=highest
    )
    out_imag = jnp.einsum("ja,...ak->...jk", left_real, half_imag, precision=highest) + jnp.einsum(
        "ja,...ak->...jk", left_imag, half_real, precision=highest
    )
    return (out_real, out_imag)


def on_device(images, anchors, patches, coeffs, zbasis):
    highest = lax.Precision.HIGHEST
    devices = lax.axis_size("sub")
    device_index = lax.axis_index("sub")
    strip_width = images.shape[3] // devices
    reach = SUB // strip_width
    column_strip = lax.all_to_all(images, "sub", split_axis=3, concat_axis=2, tiled=True)
    strip_list = [column_strip]
    for step_right in range(1, reach + 1):
        strip_list.append(from_behind(column_strip, "sub", -step_right))
    widened = jnp.concatenate(strip_list, axis=3)
    offsets = anchors - device_index * strip_width
    subfield_list = []
    for row_tile in range(TR):
        strip_rows = widened[:, :, row_tile * SUB : (row_tile + 1) * SUB, :]
        subfield_list.append(lax.dynamic_slice_in_dim(strip_rows, offsets[row_tile], SUB, 3))
    window_two = taper(SUB)[:, None] * taper(SUB)[None, :]
    subfields = jnp.stack(subfield_list, axis=2) * window_two
    full_real, full_imag = dft_tables(SUB)
    full_table = (full_real, full_imag)
    pupil_table = (full_real[:, :PUP], full_imag[:, :PUP])
    data_real, data_imag = complex_dft(subfields, None, full_table, full_table)
    power_sum = jnp.sum(data_real * data_real + data_imag * data_imag, axis=1)
    pupil_mask = aperture(PUP)
    pupil_area = jnp.sum(pupil_mask)
    ratios = 1.0 / (1.0 + 0.25 * jnp.arange(CH, dtype=jnp.float32))
    owned_count = coeffs.shape[2]
    total_patches = owned_count * devices
    selector = (patches[None, :] == jnp.arange(total_patches, dtype=jnp.int32)[:, None]).astype(
        jnp.float32
    )

    def objective(chosen):
        phases = jnp.einsum("fms,mq->fsq", chosen, zbasis, precision=highest)
        phases = phases.reshape(phases.shape[:2] + (PUP, PUP))
        scaled = ratios[:, None, None, None, None] * phases[None]
        pupil_real = pupil_mask * jnp.cos(scaled)
        pupil_imag = pupil_mask * jnp.sin(scaled)
        field_real, field_imag = complex_dft(pupil_real, pupil_imag, pupil_table, pupil_table)
        psf_values = (field_real * field_real + field_imag * field_imag) / (SUB * SUB * pupil_area)
        otf_real, otf_imag = complex_dft(psf_values, None, full_table, full_table)
        cross_real = jnp.sum(data_real * otf_real + data_imag * otf_imag, axis=1)
        cross_imag = jnp.sum(data_imag * otf_real - data_real * otf_imag, axis=1)
        denominator = jnp.sum(otf_real * otf_real + otf_imag * otf_imag, axis=1) + GAMMA
        return (
            jnp.sum(power_sum - (cross_real * cross_real + cross_imag * cross_imag) / denominator)
            / SUB**4
        )

    current = coeffs
    gradient = jnp.zeros_like(coeffs)
    for iteration in range(ITERS):
        gathered = lax.all_gather(current, "sub", axis=2, tiled=True)
        chosen = jnp.einsum("fmp,ps->fms", gathered, selector, precision=highest)
        loss_value, pullback = jax.vjp(objective, chosen)
        (slopes,) = pullback(jnp.ones_like(loss_value))
        spread = jnp.einsum("fms,ps->fmp", slopes, selector, precision=highest)
        gradient = lax.psum_scatter(spread, "sub", scatter_dimension=2, tiled=True)
        current = current - STEP_SIZE * gradient
    return (current, gradient)


def solution(mesh):
    return jax.shard_map(
        on_device,
        mesh=mesh,
        in_specs=(P(None, None, "sub", None), P("sub"), P("sub"), P(None, None, "sub"), P()),
        out_specs=(P(None, None, "sub"), P(None, None, "sub")),
        check_vma=False,
    )
```

profile of v0, /device:TPU:0, one launch (start us, length us, event | category | flops | bytes accessed | tf_op | source)
XLA Modules:
  0.0 484.9 jit_solution(7883281226299236298)
XLA Ops:
  0.6 13.1 %copy.172 = f32[2,4,16,4096]{2,1,0,3:T(4,128)} copy(f32[2,4,16,4096]{3,2,1,0:T(8,128)} %param.5) | data formatting | bytes 4194304 | tf_op args[0]
  13.7 16.4 %reshape.149 = f32[32,1,16384]{2,1,0:T(1,128)} reshape(f32[4096,2,4,16]{3,2,1,0:T(4,128)} %bitcast.273) | data formatting | bytes 4194304
  30.1 7.4 %all-to-all-start = ((f32[32,1,16384]{2,1,0:T(1,128)}), f32[32,1,16384]{2,1,0:T(1,128)}, u32[]{:S(2)}, u32[]{:S(2)}) async-start(f32[32,1,16384]{2,1,0:T(1,128)} %reshape.149), calls=%async_computation | async-start | bytes 4194304 | tf_op jit(solution)/shard_map/all_to_all | solution.py:71
  37.6 69.9 %all_gather.6 = f32[4,45,32]{1,0,2:T(4,128)S(1)} all-gather(f32[4,45,1]{1,0,2:T(4,128)S(1)} %bitcast.277), channel_id=1, replica_groups=mesh['sub'=32] {'sub'}, dimensions={2}, use_global_device_ids=true | all-gather | bytes 23760 | tf_op jit(solution)/shard_map/all_gather | solution.py:117
  111.3 4.4 fusion.52
  115.7 4.4 fusion.54
  120.1 4.5 fusion.63
  124.6 4.4 fusion.60
  132.4 3.6 fusion.349
  136.1 3.5 convolution_subtract_fusion.1
  139.6 3.4 convolution_add_fusion.1
  144.3 4.3 fusion.14
  149.1 8.7 %reduce.6 = f32[32,16384]{1,0:T(8,128)} reduce(f32[32,1,16384]{2,1,0:T(1,128)} %all-to-all-done, f32[]{:T(128)} %broadcast.349), dimensions={1}, to_apply=%all_to_all.13.reduce_sub_computation | reduce | bytes 4194308 | tf_op jit(solution)/shard_map/all_to_all | solution.py:71
  157.9 14.7 %reshape.150 = f32[4096,2,4,16]{3,2,1,0:T(4,128)} reshape(f32[32,16384]{1,0:T(8,128)} %reduce.6) | data formatting | bytes 4194304
  172.6 13.7 %copy.286 = f32[2,4,16,32,128]{4,2,3,1,0:T(8,128)} copy(f32[2,4,16,32,128]{2,1,0,4,3:T(4,128)} %bitcast.272) | data formatting | bytes 4194304 | tf_op jit(solution)/shard_map/all_to_all | solution.py:71
  195.9 3.8 fusion.169
  237.6 3.6 fusion.8
  241.2 4.9 %add_divide_fusion.2 = f32[2,4,4,128,128]{4,3,2,1,0:T(8,128)} fusion(f32[2,4,4,128,128]{4,3,2,1,0:T(8,128)S(1)} %fusion.8, f32[2,4,4,128,128]{4,3,2,1,0:T(8,128)S(1)} %fusion.159, f32[2,4,4,128,128]{4,3,2,1,0:T(8,128)S(1)} %fusion.30, f32[]{:T(128)S(6)} %mul.931), kind=kOutput, calls=%fused_computation.48 | convolution fusion | flops 807124992 | bytes 8388612 | tf_op jit(solution)/shard_map/transpose(jvp(...ab,kb->...ak))/dot_general | solution.py:48
  249.5 4.9 %fusion.104 = f32[2,4,4,128,64]{3,4,2,1,0:T(8,128)S(1)} fusion(f32[2,4,4,128,128]{3,4,2,1,0:T(8,128)} %copy.193, f32[2,4,4,128,128]{4,3,2,1,0:T(8,128)} %copy-done.7, f32[128,128]{0,1:T(8,128)S(1)} %sine_negate_fusion), kind=kOutput, calls=%fused_computation.126 | convolution fusion | flops 403701760 | bytes 5275648 | tf_op jit(solution)/shard_map/transpose(jvp(ja,...ak->...jk))/dot_general | solution.py:59
  264.0 4.4 fusion.38
  268.4 5.5 %fusion.97 = f32[4,4,64,64]{3,2,1,0:T(8,128)} fusion(f32[2,4,4,64,64]{4,3,2,1,0:T(8,128)S(1)} %fusion.38, f32[2,4,4,64,64]{4,3,2,1,0:T(8,128)S(1)} %fusion.347, f32[2,4,4,64,128]{4,3,2,1,0:T(8,128)S(1)} %fusion.91, f32[4,4,64,64]{3,2,1,0:T(8,128)S(1)} %mul.919, f32[64,64]{1,0:T(8,128)S(1)} %fusion.210, f32[2]{0:T(128)S(1)} %add_divide_fusion.6, ...), kind=kOutput, calls=%fused_computation.114 | convolution fusion | flops 202440704 | bytes 3998208 | tf_op jit(solution)/shard_map/transpose(jvp(...ab,kb->...ak))/dot_general | solution.py:50
  276.5 48.4 %all-reduce = f32[4,45,32]{1,0,2:T(4,128)S(1)} all-reduce(f32[4,45,32]{1,0,2:T(4,128)S(1)} %copy.194), channel_id=2, replica_groups=mesh['sub'=32] {'sub'}, use_global_device_ids=true, to_apply=%region_5.6.clone | all-reduce | flops 5760 | bytes 46080
  325.0 40.5 %all_gather.7 = f32[4,45,32]{1,0,2:T(4,128)S(1)} all-gather(f32[4,45,1]{1,0,2:T(4,128)S(1)} %fusion.212), channel_id=1, replica_groups=mesh['sub'=32] {'sub'}, dimensions={2}, use_global_device_ids=true | all-gather | bytes 23760 | tf_op jit(solution)/shard_map/all_gather | solution.py:117
  368.2 4.4 fusion.44
  372.6 5.1 %fusion.46 = f32[2,4,4,64,128]{4,3,2,1,0:T(8,128)S(1)} fusion(f32[4,4,64,64]{3,2,1,0:T(8,128)S(1)} %mul.967, f32[64,64]{1,0:T(8,128)S(1)} %fusion.210, f32[2]{0:T(128)S(1)} %add_divide_fusion.6, f32[128,128]{0,1:T(8,128)} %copy-done.11), kind=kOutput, calls=%fused_computation.80 | convolution fusion | flops 201588736 | bytes 1359880 | tf_op jit(solution)/shard_map/jvp(...ab,kb->...ak)/dot_general | solution.py:53
  377.7 4.7 fusion.69
  384.3 4.3 fusion.66
  419.2 3.6 fusion
  422.8 3.6 add_divide_fusion
  434.4 4.2 fusion.42
  438.6 5.7 %fusion.96 = f32[4,4,64,64]{3,2,1,0:T(8,128)} fusion(f32[2,4,4,64,64]{4,3,2,1,0:T(8,128)S(1)} %fusion.42, f32[2,4,4,64,64]{4,3,2,1,0:T(8,128)S(1)} %fusion.344, f32[2,4,4,64,128]{4,3,2,1,0:T(8,128)S(1)} %fusion.87, f32[4,4,64,64]{3,2,1,0:T(8,128)S(1)} %mul.967, f32[64,64]{1,0:T(8,128)S(1)} %fusion.210, f32[2]{0:T(128)S(1)} %add_divide_fusion.6, ...), kind=kOutput, calls=%fused_computation.113 | convolution fusion | flops 202440704 | bytes 3998208 | tf_op jit(solution)/shard_map/transpose(jvp(...ab,kb->...ak))/dot_general | solution.py:50
  446.9 37.2 %all-reduce.1 = f32[4,45,32]{1,0,2:T(4,128)S(1)} all-reduce(f32[4,45,32]{1,0,2:T(4,128)S(1)} %copy.224), channel_id=3, replica_groups=mesh['sub'=32] {'sub'}, use_global_device_ids=true, to_apply=%region_10.11.clone | all-reduce | flops 5760 | bytes 46080
  (115 shorter events, 109.5 us)
Async XLA Ops:
  0.6 107.1 %copy-start = (f32[45,4096]{1,0:T(8,128)S(1)}, f32[45,4096]{1,0:T(8,128)}, u32[]{:S(2)}) copy-start(f32[45,4096]{1,0:T(8,128)} %param.9) | copy-start | bytes 2211844
  30.1 7.5 %copy-start.15 = (f32[4,45,1]{1,2,0:T(1,128)S(1)}, f32[4,45,1]{1,2,0:T(1,128)}, u32[]{:S(2)}) copy-start(f32[4,45,1]{1,2,0:T(1,128)} %param.8) | copy-start | bytes 2164
  30.1 77.4 %copy-start.16 = (s32[4]{0:T(128)S(1)}, s32[4]{0:T(128)}, u32[]{:S(2)}) copy-start(s32[4]{0:T(128)} %param.7) | copy-start | bytes 52
  30.1 118.5 %all-to-all-start = ((f32[32,1,16384]{2,1,0:T(1,128)}), f32[32,1,16384]{2,1,0:T(1,128)}, u32[]{:S(2)}, u32[]{:S(2)}) async-start(f32[32,1,16384]{2,1,0:T(1,128)} %reshape.149), calls=%async_computation | async-start | bytes 4194304 | tf_op jit(solution)/shard_map/all_to_all | solution.py:71
  37.6 72.9 %copy-start.17 = (s32[4]{0:T(128)S(1)}, s32[4]{0:T(128)}, u32[]{:S(2)}) copy-start(s32[4]{0:T(128)} %param.6) | copy-start | bytes 52
  110.5 21.9 %copy-start.11 = (f32[128,128]{0,1:T(8,128)}, f32[128,128]{0,1:T(8,128)S(1)}, u32[]{:S(2)}) copy-start(f32[128,128]{0,1:T(8,128)S(1)} %fusion.194) | copy-start | bytes 196612
  139.6 60.1 %copy-start.4 = (f32[2,4,4,128,128]{4,3,2,1,0:T(8,128)}, f32[2,4,4,128,128]{4,3,2,1,0:T(8,128)S(1)}, u32[]{:S(2)}) copy-start(f32[2,4,4,128,128]{4,3,2,1,0:T(8,128)S(1)} %convolution_subtract_fusion.1) | copy-start | bytes 6291460
  143.0 1.3 copy-start.7
  186.3 22.5 %collective-permute-start = (f32[2,4,512,128]{3,2,1,0:T(8,128)}, f32[2,4,512,128]{3,2,1,0:T(8,128)}, u32[]{:S(2)}, u32[]{:S(2)}) collective-permute-start(f32[2,4,512,128]{3,2,1,0:T(8,128)} %bitcast.274), channel_id=1, source_target_pairs={{1,0},{2,1},{3,2},{4,3},{5,4},{6,5},{7,6},{8,7},{9,8},{10,9},{11,1... | collective-permute-start | bytes 6291464 | tf_op jit(solution)/shard_map/ppermute | solution.py:22
  195.9 3.8 copy-start.8
  204.3 2.1 copy-start.10
  206.4 2.1 copy-start.6
  211.3 1.7 copy-start.14
  227.2 2.0 copy-start.2
  249.4 4.9 %copy-start.1 = (f32[2,4,4,128,128]{3,4,2,1,0:T(8,128)S(1)}, f32[2,4,4,128,128]{3,4,2,1,0:T(8,128)}, u32[]{:S(2)}) copy-start(f32[2,4,4,128,128]{3,4,2,1,0:T(8,128)} %copy.193) | copy-start | bytes 6291460
  249.4 4.9 %copy-start.9 = (f32[2,4,4,128,128]{4,3,2,1,0:T(8,128)S(1)}, f32[2,4,4,128,128]{4,3,2,1,0:T(8,128)}, u32[]{:S(2)}) copy-start(f32[2,4,4,128,128]{4,3,2,1,0:T(8,128)} %copy-done.7) | copy-start | bytes 6291460
  249.4 4.9 %copy-start.12 = (f32[128,128]{0,1:T(8,128)S(1)}, f32[128,128]{0,1:T(8,128)}, u32[]{:S(2)}) copy-start(f32[128,128]{0,1:T(8,128)} %copy-done.11) | copy-start | bytes 196612
  254.4 2.5 copy-start.5
  368.2 9.5 %copy-start.13 = (f32[128,128]{0,1:T(8,128)S(1)}, f32[128,128]{0,1:T(8,128)}, u32[]{:S(2)}) copy-start(f32[128,128]{0,1:T(8,128)} %copy-done.11) | copy-start | bytes 196612
  403.6 2.3 copy-start.3
where the time goes:
time: 490 us; the launch traced here: 485 us
  blocking collectives  196 us (40%)
  matrix products  182 us (37%)
  local copies, waits for them, and re-layouts  69.9 us (14%)
  other arithmetic  17.9 us (4%)
  between operations  9.92 us (2%)
  starting transfers between devices  8.88 us (2%)
    all_gather x2, blocking collectives, on_device(): gathered = lax.all_gather(current, 'sub', axis=2, tiled=True)  110 us
    unnamed x2, blocking collectives  85.6 us
    unnamed x39, local copies, waits for them, and re-layouts  45.6 us
    dot_general x9, matrix products, complex_dft(): jnp.einsum('...ab,kb->...ak', real_part, right_real, precision=highest)  32.5 us
    dot_general x9, matrix products, complex_dft(): jnp.einsum('...ab,kb->...ak', real_part, right_imag, precision=highest)  28.4 us
    dot_general x9, matrix products, complex_dft(): jnp.einsum('ja,...ak->...jk', left_imag, half_real, precision=highest)  22.5 us
    dot_general x9, matrix products, complex_dft(): jnp.einsum('ja,...ak->...jk', left_real, half_imag, precision=highest)  21.7 us
    dot_general x9, matrix products, complex_dft(): jnp.einsum('ja,...ak->...jk', left_imag, half_imag, precision=highest)  21.3 us
  transfers between devices with their start and end apart: 2, of which 0 were waited for; matrix products, arithmetic and copies ran while one was open for 11% of the time, Pallas kernels for 0%

commit v1 on v0

v1 whole, which is shorter than its diff:
```python
import functools
import math

import jax
import jax.numpy as jnp
import ml_dtypes
import numpy as np
from jax import lax
from jax.experimental import pallas as pl
from jax.experimental.pallas import tpu as pltpu
from jax.sharding import PartitionSpec as P

SUB = 128
CH = 2
FRAMES = 4
TR = 4
ITERS = 2
PUP = 64
HALF = 72
GAMMA = 0.01
STEP_SIZE = 0.05
F32 = jnp.float32
BF16 = jnp.bfloat16
VMEM_LIMIT = 48 << 20
HIGHEST = lax.Precision.HIGHEST


def split_np(matrix):
    matrix = np.asarray(matrix, np.float32)
    high = matrix.astype(ml_dtypes.bfloat16)
    low = (matrix - high.astype(np.float32)).astype(ml_dtypes.bfloat16)
    return high, low


def make_tables():
    k = np.arange(SUB)
    angle = 2.0 * np.pi * (np.outer(k, k) % SUB) / SUB
    cos, sin = np.cos(angle), np.sin(angle)
    taper = 0.5 - 0.5 * np.cos(2.0 * np.pi * (k + 0.5) / SUB)
    right = np.zeros((2, 2, PUP, 2, 2, SUB))
    for half in range(2):
        right[0, half, :, half, 0] = cos[:PUP]
        right[0, half, :, half, 1] = -sin[:PUP]
        right[1, half, :, half, 0] = sin[:PUP]
        right[1, half, :, half, 1] = cos[:PUP]
    right = right.reshape(2 * SUB, 4 * SUB)
    left = np.block([[cos[:, :PUP], sin[:, :PUP]], [-sin[:, :PUP], cos[:, :PUP]]])
    rows_cos, rows_sin = np.zeros((HALF, SUB)), np.zeros((HALF, SUB))
    rows_cos[:65], rows_sin[:65] = cos[:65], sin[:65]
    rows = np.concatenate([rows_cos, rows_sin], 0)
    mixed = np.block([[cos, -sin], [-sin, -cos]])
    weight = np.zeros((HALF, 1))
    weight[:65] = 2.0
    weight[0] = weight[64] = 1.0
    centred = np.arange(PUP) - PUP / 2 + 0.5
    mask = (centred[:, None] ** 2 + centred[None, :] ** 2 <= (PUP / 2) ** 2).astype(np.float32)
    area = float(mask.sum())
    mask = mask.reshape(2, PUP // 2, PUP).transpose(1, 0, 2).reshape(PUP // 2, SUB)
    return {
        "right": right,
        "right_t": right.T,
        "left": left,
        "left_t": left.T,
        "rows": rows,
        "rows_t": rows.T,
        "mixed": mixed,
        "data_rows": rows * taper[None, :],
        "data_mixed": np.concatenate([taper, taper])[:, None] * mixed,
        "weight": np.broadcast_to(weight, (HALF, SUB)).astype(np.float32) * np.float32(-2.0 / SUB**4),
        "mask": np.tile(mask, (FRAMES, 1)),
        "area": area,
    }


def split(value):
    high = value.astype(BF16)
    low = (value - high.astype(F32)).astype(BF16)
    return high, low


def dot(a, b):
    return jnp.dot(a, b, preferred_element_type=F32)


def const_left(high_ref, low_ref, value):
    high, low = split(value)
    table = high_ref[...]
    return dot(table, high) + (dot(table, low) + dot(low_ref[...], high))


def const_right(value, high_ref, low_ref):
    high, low = split(value)
    table = high_ref[...]
    return dot(high, table) + (dot(low, table) + dot(high, low_ref[...]))


def sin_cos(angle):
    turns = jnp.floor(angle * np.float32(2.0 / math.pi) + 0.5)
    rest = angle - turns * np.float32(1.5703125)
    rest = rest - turns * np.float32(4.8351287841796875e-4)
    rest = rest - turns * np.float32(3.1385570764541626e-7)
    rest = rest - turns * np.float32(6.0771005065061922e-11)
    square = rest * rest
    sine = rest + rest * square * (
        -1.6666654611e-1 + square * (8.3321608736e-3 + square * -1.9515295891e-4)
    )
    cosine = 1.0 - 0.5 * square + square * square * (
        4.166664568298827e-2 + square * (-1.388731625493765e-3 + square * 2.443315711809948e-5)
    )
    quadrant = turns - 4.0 * jnp.floor(turns * 0.25)
    odd = (quadrant == 1.0) | (quadrant == 3.0)
    base_sin = jnp.where(odd, cosine, sine)
    base_cos = jnp.where(odd, sine, cosine)
    out_sin = jnp.where(quadrant >= 2.0, -base_sin, base_sin)
    out_cos = jnp.where((quadrant == 1.0) | (quadrant == 2.0), -base_cos, base_cos)
    return out_sin, out_cos


def half_plane(images, rows_high, rows_low, mixed_high, mixed_low):
    columns = const_left(rows_high, rows_low, images)
    stacked = jnp.concatenate(
        [
            jnp.concatenate(
                [columns[:HALF, f * SUB : (f + 1) * SUB], columns[HALF:, f * SUB : (f + 1) * SUB]], 1
            )
            for f in range(FRAMES)
        ],
        0,
    )
    return const_right(stacked, mixed_high, mixed_low)


def window_kernel(anchor_ref, image_ref, out_ref):
    anchor = anchor_ref[pl.program_id(0)]
    last = image_ref.shape[1] - SUB
    base = pl.multiple_of((anchor // SUB) * SUB, SUB)
    after = pl.multiple_of(jnp.minimum(base + SUB, last), SUB)
    shift = anchor - base
    first = image_ref[:, pl.ds(base, SUB)]
    second = image_ref[:, pl.ds(after, SUB)]
    second = jnp.where(base + SUB <= last, second, 0.0)
    both = jnp.concatenate([first, second], 1)
    out_ref[0] = pltpu.roll(both, 2 * SUB - shift, 1)[:, :SUB]


def data_kernel(cells_ref, rows_high, rows_low, mixed_high, mixed_low, out_ref):
    images = jnp.concatenate([cells_ref[0, f] for f in range(FRAMES)], 1)
    out_ref[0, 0] = half_plane(images, rows_high, rows_low, mixed_high, mixed_low)


def forward_kernel(
    scale,
    modes,
    coeff_ref,
    basis_ref,
    mask_ref,
    right_high,
    right_low,
    left_high,
    left_low,
    rows_high,
    rows_low,
    mixed_high,
    mixed_low,
    otf_ref,
    field_ref,
    pupil_ref,
):
    subfield = pl.program_id(0)
    channel = pl.program_id(1)
    ratio = 1.0 / (1.0 + 0.25 * channel.astype(F32))
    sums = [jnp.zeros((PUP // 2, SUB), F32) for _ in range(FRAMES)]
    for m in range(modes):
        mode = basis_ref[m]
        for f in range(FRAMES):
            sums[f] = sums[f] + coeff_ref[subfield * FRAMES + f, m] * mode
    phase = jnp.concatenate(sums, 0) * ratio
    sine, cosine = sin_cos(phase)
    mask = mask_ref[...]
    pupil = jnp.concatenate([mask * cosine, mask * sine], 1)
    pupil_ref[0, 0] = pupil
    half = const_right(pupil, right_high, right_low)
    q = PUP // 2
    blocks = jnp.concatenate(
        [
            jnp.concatenate(
                [half[f * q : (f + 1) * q, n * SUB : (n + 1) * SUB] for n in (0, 2, 1, 3)], 0
            )
            for f in range(FRAMES)
        ],
        1,
    )
    field = const_left(left_high, left_low, blocks)
    field_ref[0, 0] = field
    psf = (field[:SUB] * field[:SUB] + field[SUB:] * field[SUB:]) * scale
    otf_ref[0, 0] = half_plane(psf, rows_high, rows_low, mixed_high, mixed_low)


def backward_kernel(
    scale,
    data_ref,
    otf_ref,
    field_ref,
    pupil_ref,
    basis_ref,
    weight_ref,
    mixed_high,
    mixed_low,
    rows_high,
    rows_low,
    left_high,
    left_low,
    right_high,
    right_low,
    out_ref,
    phase_acc,
):
    channel = pl.program_id(1)
    ratio = 1.0 / (1.0 + 0.25 * channel.astype(F32))
    data = [data_ref[0, 0, f * HALF : (f + 1) * HALF, :] for f in range(FRAMES)]
    otf = [otf_ref[0, 0, f * HALF : (f + 1) * HALF, :] for f in range(FRAMES)]
    cross_real = cross_imag = power = None
    for f in range(FRAMES):
        dr, di = data[f][:, :SUB], data[f][:, SUB:]
        orr, oi = otf[f][:, :SUB], otf[f][:, SUB:]
        terms = (dr * orr + di * oi, di * orr - dr * oi, orr * orr + oi * oi)
        if f == 0:
            cross_real, cross_imag, power = terms
        else:
            cross_real = cross_real + terms[0]
            cross_imag = cross_imag + terms[1]
            power = power + terms[2]
    inverse = 1.0 / (power + GAMMA)
    slope = weight_ref[...] * inverse
    xr, xi = cross_real * inverse, cross_imag * inverse
    share = weight_ref[...] * (xr * xr + xi * xi)
    cross_real, cross_imag = cross_real * slope, cross_imag * slope
    bars = []
    for f in range(FRAMES):
        dr, di = data[f][:, :SUB], data[f][:, SUB:]
        orr, oi = otf[f][:, :SUB], otf[f][:, SUB:]
        bar_real = cross_real * dr + cross_imag * di - share * orr
        bar_imag = cross_real * di - cross_imag * dr - share * oi
        bars.append(jnp.concatenate([bar_real, bar_imag], 1))
    columns = const_right(jnp.concatenate(bars, 0), mixed_high, mixed_low)
    stacked = jnp.concatenate(
        [
            jnp.concatenate(
                [columns[f * HALF : (f + 1) * HALF, :SUB], columns[f * HALF : (f + 1) * HALF, SUB:]], 0
            )
            for f in range(FRAMES)
        ],
        1,
    )
    psf_bar = const_left(rows_high, rows_low, stacked) * (2.0 * scale)
    field = field_ref[0, 0]
    field_bar = jnp.concatenate([field[:SUB] * psf_bar, field[SUB:] * psf_bar], 0)
    half_bar = const_left(left_high, left_low, field_bar)
    q = PUP // 2
    rows = jnp.concatenate(
        [
            jnp.concatenate(
                [half_bar[n * q : (n + 1) * q, f * SUB : (f + 1) * SUB] for n in (0, 2, 1, 3)], 1
            )
            for f in range(FRAMES)
        ],
        0,
    )
    pupil_bar = const_right(rows, right_high, right_low)
    pupil = pupil_ref[0, 0]
    phase_bar = ratio * (pupil[:, :SUB] * pupil_bar[:, SUB:] - pupil[:, SUB:] * pupil_bar[:, :SUB])

    @pl.when(channel == 0)
    def _():
        phase_acc[...] = phase_bar

    @pl.when(channel == CH - 1)
    def _():
        total = phase_acc[...] + phase_bar
        modes = basis_ref.shape[0]
        ones = jnp.ones((8, SUB), F32)
        for f in range(FRAMES):
            part = jnp.sum(basis_ref[...] * total[f * q : (f + 1) * q][None], axis=1)
            line = lax.dot_general(
                ones, part, (((1,), (1,)), ((), ())), precision=HIGHEST, preferred_element_type=F32
            )
            out_ref[0, f : f + 1, :] = jnp.concatenate(
                [line[:1], jnp.zeros((1, SUB - modes), F32)], 1
            )


def gather_kernel(n, block_ref, out_ref, send_sem, recv_sem):
    me = lax.axis_index("sub")
    barrier = pltpu.get_barrier_semaphore()

    def greet(step, carry):
        pl.semaphore_signal(
            barrier,
            inc=1,
            device_id=(lax.rem(me + step, n),),
            device_id_type=pl.DeviceIdType.MESH,
        )
        return carry

    lax.fori_loop(1, n, greet, 0)
    pl.semaphore_wait(barrier, n - 1)

    def copy_to(step):
        return pltpu.make_async_remote_copy(
            src_ref=block_ref,
            dst_ref=out_ref.at[me],
            send_sem=send_sem.at[step],
            recv_sem=recv_sem.at[step],
            device_id=(lax.rem(me + step, n),),
            device_id_type=pl.DeviceIdType.MESH,
        )

    def begin(step, carry):
        copy_to(step).start()
        return carry

    def finish(step, carry):
        copy_to(step).wait()
        return carry

    lax.fori_loop(1, n, begin, 0)
    out_ref[me] = block_ref[...]
    lax.fori_loop(1, n, finish, 0)


def spread_blocks(block, ident):
    n = lax.axis_size("sub")
    return pl.pallas_call(
        functools.partial(gather_kernel, n),
        out_shape=jax.ShapeDtypeStruct((n,) + block.shape, F32),
        in_specs=[pl.BlockSpec(memory_space=pltpu.VMEM)],
        out_specs=pl.BlockSpec(memory_space=pltpu.VMEM),
        scratch_shapes=[pltpu.SemaphoreType.DMA((n,)), pltpu.SemaphoreType.DMA((n,))],
        compiler_params=pltpu.CompilerParams(collective_id=ident, has_side_effects=True),
    )(block)


def whole(array):
    return pl.BlockSpec(array.shape, lambda *_: (0,) * array.ndim, pipeline_mode=pl.Buffered(1))


def on_device(images, anchors, patches, coeffs, zbasis):
    devices = lax.axis_size("sub")
    device = lax.axis_index("sub")
    rows = images.shape[2]
    per = anchors.shape[0]
    owned = coeffs.shape[2]
    modes = coeffs.shape[1]
    tables = make_tables()
    pairs = {
        name: [jnp.asarray(part) for part in split_np(tables[name])]
        for name in tables
        if name not in ("weight", "mask", "area")
    }
    scale = float(1.0 / (SUB * SUB * tables["area"]))

    owned_rows = owned * FRAMES
    tile_rows = -(-(owned_rows + 2) // 8) * 8
    mine = jnp.zeros((tile_rows, SUB), F32)
    mine = mine.at[:owned_rows, :modes].set(coeffs.transpose(2, 0, 1).reshape(owned_rows, modes))
    mine = mine.at[owned_rows, :per].set(patches.astype(F32))
    mine = mine.at[owned_rows + 1, :per].set(anchors.astype(F32))
    everyone = spread_blocks(mine, 0)
    all_coeffs = everyone[:, :owned_rows, :].reshape(devices * owned, FRAMES * SUB)
    all_patches = everyone[:, owned_rows, :per].reshape(devices * per).astype(jnp.int32)
    tile = (device * rows) // SUB
    tile_anchors = lax.dynamic_index_in_dim(everyone[:, owned_rows + 1, :], tile, 1, keepdims=False)
    tile_anchors = tile_anchors.astype(jnp.int32)

    bands = images.reshape(CH * FRAMES * rows, images.shape[3])
    windows = pl.pallas_call(
        window_kernel,
        grid_spec=pltpu.PrefetchScalarGridSpec(
            num_scalar_prefetch=1,
            grid=(devices,),
            in_specs=[pl.BlockSpec(bands.shape, lambda j, a: (0, 0), pipeline_mode=pl.Buffered(1))],
            out_specs=pl.BlockSpec((1, bands.shape[0], SUB), lambda j, a: (j, 0, 0)),
        ),
        out_shape=jax.ShapeDtypeStruct((devices, bands.shape[0], SUB), F32),
        compiler_params=pltpu.CompilerParams(vmem_limit_bytes=VMEM_LIMIT),
    )(tile_anchors, bands)
    received = lax.all_to_all(windows, "sub", 0, 0, tiled=True)
    cells = received.reshape(TR, devices // TR, CH * FRAMES, rows, SUB)
    cells = cells.transpose(0, 2, 1, 3, 4).reshape(TR, CH * FRAMES, SUB, SUB)

    big = pltpu.CompilerParams(vmem_limit_bytes=VMEM_LIMIT)
    spectrum_shape = jax.ShapeDtypeStruct((per, CH, FRAMES * HALF, 2 * SUB), F32)

    def per_block(*tail):
        return pl.BlockSpec((1, 1) + tail, lambda s, c: (s, c, 0, 0))

    data_tables = pairs["data_rows"] + pairs["data_mixed"]
    data = pl.pallas_call(
        data_kernel,
        grid=(per, CH),
        in_specs=[pl.BlockSpec((1, FRAMES, SUB, SUB), lambda s, c: (s, c, 0, 0))]
        + [whole(t) for t in data_tables],
        out_specs=per_block(FRAMES * HALF, 2 * SUB),
        out_shape=spectrum_shape,
        compiler_params=big,
        cost_estimate=pl.CostEstimate(flops=6 * 10**9, bytes_accessed=5 << 20, transcendentals=0),
    )(cells, *data_tables)

    basis = zbasis.reshape(modes, 2, PUP // 2, PUP).transpose(0, 2, 1, 3).reshape(modes, PUP // 2, SUB)
    mask = jnp.asarray(tables["mask"])
    weight = jnp.asarray(tables["weight"])
    forward_tables = pairs["right"] + pairs["left"] + pairs["rows"] + pairs["mixed"]
    backward_tables = pairs["mixed"] + pairs["rows_t"] + pairs["left_t"] + pairs["right_t"]
    saved_shapes = [
        spectrum_shape,
        jax.ShapeDtypeStruct((per, CH, 2 * SUB, FRAMES * SUB), F32),
        jax.ShapeDtypeStruct((per, CH, FRAMES * PUP // 2, 2 * SUB), F32),
    ]
    saved_specs = [per_block(*s.shape[2:]) for s in saved_shapes]

    def slopes_of(chosen):
        flat = chosen.reshape(per * FRAMES, SUB)
        saved = pl.pallas_call(
            functools.partial(forward_kernel, scale, modes),
            grid=(per, CH),
            in_specs=[pl.BlockSpec(memory_space=pltpu.SMEM), whole(basis), whole(mask)]
            + [whole(t) for t in forward_tables],
            out_specs=saved_specs,
            out_shape=saved_shapes,
            compiler_params=big,
            cost_estimate=pl.CostEstimate(flops=10**10, bytes_accessed=8 << 20, transcendentals=0),
        )(flat, basis, mask, *forward_tables)
        return pl.pallas_call(
            functools.partial(backward_kernel, scale),
            grid=(per, CH),
            in_specs=[per_block(FRAMES * HALF, 2 * SUB)]
            + saved_specs
            + [whole(basis), whole(weight)]
            + [whole(t) for t in backward_tables],
            out_specs=pl.BlockSpec((1, FRAMES, SUB), lambda s, c: (s, 0, 0)),
            out_shape=jax.ShapeDtypeStruct((per, FRAMES, SUB), F32),
            scratch_shapes=[pltpu.VMEM((FRAMES * PUP // 2, SUB), F32)],
            compiler_params=big,
            cost_estimate=pl.CostEstimate(flops=10**10, bytes_accessed=8 << 20, transcendentals=0),
        )(data, *saved, basis, weight, *backward_tables)

    patch_ids = jnp.arange(devices * owned, dtype=jnp.int32)
    own_ids = device * owned + jnp.arange(owned, dtype=jnp.int32)
    wanted = jnp.concatenate([patches, own_ids])
    picks = (wanted[:, None] == patch_ids[None, :]).astype(F32)
    current = jnp.dot(picks, all_coeffs, precision=HIGHEST)
    sums = (wanted[:, None] == all_patches[None, :]).astype(F32)
    gradient = jnp.zeros_like(current)
    for iteration in range(ITERS):
        slopes = slopes_of(current[:per])
        gathered = spread_blocks(slopes.reshape(per * FRAMES, SUB), 1 + iteration)
        gathered = gathered.reshape(devices * per, FRAMES * SUB)
        gradient = jnp.dot(sums, gathered, precision=HIGHEST)
        current = current - STEP_SIZE * gradient

    def owned_part(value):
        return value[per:].reshape(owned, FRAMES, SUB)[:, :, :modes].transpose(1, 2, 0)

    return owned_part(current), owned_part(gradient)


def solution(mesh):
    return jax.shard_map(
        on_device,
        mesh=mesh,
        in_specs=(P(None, None, "sub", None), P("sub"), P("sub"), P(None, None, "sub"), P()),
        out_specs=(P(None, None, "sub"), P(None, None, "sub")),
        check_vma=False,
    )
```

time: 490 us -> 164 us (0.33)
  blocking collectives: 196 us -> 0 us
  matrix products: 182 us -> 0.62 us
  Pallas kernels: 0 us -> 107 us
  local copies, waits for them, and re-layouts: 69.9 us -> 18.6 us
  waiting for transfers between devices: 0.01 us -> 27.9 us
  other arithmetic: 17.9 us -> 2.79 us
  between operations: 9.92 us -> 1.1 us
    dot_general x70 -> x3, matrix products: 182 us -> 0.62 us  [the longest x2 0.43 us: on_device(): gradient = jnp.dot(sums, gathered, precision=HIGHEST)]
    all_gather x2 -> x0, blocking collectives: 110 us -> none  [on_device(): gathered = lax.all_gather(current, 'sub', axis=2, tiled=True)]
    pallas_call x0 -> x9, Pallas kernels: none -> 107 us  [the longest x3 35.6 us: spread_blocks(): pl.pallas_call(functools.partial(gather_kernel, n), out_shape=jax.ShapeDt...]
    unnamed x2 -> x0, blocking collectives: 85.6 us -> none
    unnamed x39 -> x66, local copies, waits for them, and re-layouts: 45.6 us -> 7.43 us
    all_to_all x1, waiting for transfers between devices: 0.01 us -> 27.9 us  [on_device(): received = lax.all_to_all(windows, 'sub', 0, 0, tiled=True)]
    all_to_all x2 -> x0, local copies, waits for them, and re-layouts: 14.2 us -> none  [on_device(): lax.all_to_all(images, 'sub', split_axis=3, concat_axis=2, tiled=True)]
    all_to_all x1 -> x0, other arithmetic: 8.74 us -> none  [on_device(): lax.all_to_all(images, 'sub', split_axis=3, concat_axis=2, tiled=True)]
  transfers between devices with their start and end apart: 2 -> 1, of which waited for: 0 -> 1; matrix products, arithmetic and copies ran while one was open for 11% -> 3% of each run, Pallas kernels for 0% -> 8%
where the time goes in v1:
time: 164 us
  Pallas kernels  107 us (65%)
  waiting for transfers between devices  27.9 us (17%)
  local copies, waits for them, and re-layouts  18.6 us (11%)
  starting transfers between devices  6.07 us (4%)
  other arithmetic  2.79 us (2%)
    pallas_call x3, Pallas kernels, spread_blocks(): pl.pallas_call(functools.partial(gather_kernel, n), out_shape=jax.ShapeDt...  35.6 us
    pallas_call x2, Pallas kernels, slopes_of(): pl.pallas_call(functools.partial(backward_kernel, scale), grid=(per, CH),...  29 us
    all_to_all x1, waiting for transfers between devices, on_device(): received = lax.all_to_all(windows, 'sub', 0, 0, tiled=True)  27.9 us
    pallas_call x2, Pallas kernels, slopes_of(): pl.pallas_call(functools.partial(forward_kernel, scale, modes), grid=(per...  25.3 us
    pallas_call x1, Pallas kernels, on_device(): pl.pallas_call(window_kernel, grid_spec=pltpu.PrefetchScalarGridSpec(num_...  12.4 us
    unnamed x66, local copies, waits for them, and re-layouts  7.43 us
    all_to_all x1, starting transfers between devices, on_device(): received = lax.all_to_all(windows, 'sub', 0, 0, tiled=True)  6.07 us
    reshape x3, local copies, waits for them, and re-layouts, on_device(): zbasis.reshape(modes, 2, PUP // 2, PUP).transpose(0, 2, 1, 3)  5.26 us
  transfers between devices with their start and end apart: 1, of which 1 were waited for; matrix products, arithmetic and copies ran while one was open for 3% of the time, Pallas kernels for 8%

profile of v1, /device:TPU:0, one launch (start us, length us, event | category | flops | bytes accessed | tf_op | source)
XLA Modules:
  0.0 163.7 jit_solution(17676265460213140142)
XLA Ops:
  0.6 0.7 convert_bitcast_fusion
  1.3 0.7 convert_bitcast_fusion.1
  2.0 0.7 scatter.10
  3.0 0.6 copy-done.31
  3.5 11.9 %shard_map.248 = f32[32,8,128]{2,1,0:T(8,128)} custom-call(f32[8,128]{1,0:T(8,128)} %copy-done.31), custom_call_target="tpu_custom_call" | custom-call | tf_op jit(solution)/shard_map/pallas_call | solution.py:333
  15.5 0.9 slice.87
  16.4 0.7 convert_reduce_fusion.anchor_ref
  17.2 1.6 copy-done
  18.8 12.4 %shard_map.249 = f32[32,128,128]{2,1,0:T(8,128)} custom-call(s32[32]{0:T(128)S(1)} %convert_reduce_fusion.anchor_ref, f32[128,4096]{1,0:T(8,128)S(1)} %bitcast.28), custom_call_target="tpu_custom_call" | custom-call | tf_op jit(solution)/shard_map/pallas_call | solution.py:376
  31.1 6.1 %all-to-all-start = ((f32[32,128,128]{2,1,0:T(8,128)}), f32[32,128,128]{2,1,0:T(8,128)}, u32[]{:S(2)}, u32[]{:S(2)}) async-start(f32[32,128,128]{2,1,0:T(8,128)} %shard_map.249), calls=%async_computation | async-start | bytes 4194304 | tf_op jit(solution)/shard_map/all_to_all | solution.py:387
  37.7 1.7 %reshape.155 = f32[45,2,32,64]{3,2,1,0:T(8,128)} reshape(f32[45,4096]{1,0:T(8,128)S(1)} %copy-done.29) | data formatting | bytes 1474560 | tf_op jit(solution)/shard_map/reshape | solution.py:409
  39.5 2.7 %copy.37 = f32[45,2,32,64]{3,1,2,0:T(2,128)S(1)} copy(f32[45,2,32,64]{3,2,1,0:T(8,128)} %reshape.155) | data formatting | bytes 1474560 | tf_op jit(solution)/shard_map/reshape | solution.py:409
  42.2 0.8 reshape.156.basis_ref
  43.1 12.7 %shard_map.251 = (f32[4,2,288,256]{3,2,1,0:T(8,128)S(1)}, f32[4,2,256,512]{3,2,1,0:T(8,128)}, f32[4,2,128,256]{3,2,1,0:T(8,128)S(1)}) custom-call(f32[16,128]{1,0:T(8,128)S(1)} %reshape.154.coeff_ref, f32[45,32,128]{2,1,0:T(8,128)S(1)} %reshape.156.basis_ref, f32[128,128]{1,0:T(8,128)S(1)} %copy-done.15, bf16[256,512]{1,0:T(8,128)(2,1)S(1)} %copy-done.6, ...), custom_call_target="tpu_custom_call" | custom-call | flops 10000000000 | bytes 8388608 | tf_op jit(solution)/shard_map/pallas_call | solution.py:423
  55.8 1.5 copy-done.26
  57.2 1.0 copy-done.27
  58.2 27.9 %all-to-all-done = f32[32,128,128]{2,1,0:T(8,128)} async-done(((f32[32,128,128]{2,1,0:T(8,128)}), f32[32,128,128]{2,1,0:T(8,128)}, u32[]{:S(2)}, u32[]{:S(2)}) %all-to-all-start) | async-done | bytes 2097184 | tf_op jit(solution)/shard_map/all_to_all | solution.py:387
  86.1 1.9 %copy.29 = f32[4,8,8,16,128]{4,3,1,2,0:T(8,128)S(1)} copy(f32[4,8,8,16,128]{4,3,2,1,0:T(8,128)} %bitcast.5) | data formatting | bytes 4194304 | tf_op jit(solution)/shard_map/reshape | solution.py:388
  88.1 4.4 %shard_map.250.data_ref = f32[4,2,288,256]{3,2,1,0:T(8,128)S(1)} custom-call(f32[4,8,128,128]{3,2,1,0:T(8,128)S(1)} %bitcast.29, bf16[144,128]{1,0:T(8,128)(2,1)S(1)} %copy-done.22, bf16[144,128]{1,0:T(8,128)(2,1)S(1)} %copy-done.21, bf16[256,256]{1,0:T(8,128)(2,1)S(1)} %copy-done.10, bf16[256,256]{1,0:T(8,128)(2,1)S(1)} %copy-done.9), custom_call_target="tpu_custom_call" | custom-call | flops 6000000000 | bytes 5242880 | tf_op jit(solution)/shard_map/pallas_call | solution.py:398
  92.7 14.8 %shard_map.252 = f32[4,4,128]{2,1,0:T(4,128)S(1)} custom-call(f32[4,2,288,256]{3,2,1,0:T(8,128)S(1)} %shard_map.250.data_ref, f32[4,2,288,256]{3,2,1,0:T(8,128)} %copy-done.26, f32[4,2,256,512]{3,2,1,0:T(8,128)} %get-tuple-element.45.field_ref, f32[4,2,128,256]{3,2,1,0:T(8,128)S(1)} %copy-done.28, f32[45,32,128]{2,1,0:T(8,128)S(1)} %reshape.156.basis_ref, ...), custom_call_target="tpu_custom_call" | custom-call | flops 10000000000 | bytes 8388608 | tf_op jit(solution)/shard_map/pallas_call | solution.py:433
  107.5 0.6 copy-done.2
  108.1 10.4 %shard_map.253 = f32[32,16,128]{2,1,0:T(8,128)} custom-call(f32[16,128]{1,0:T(8,128)} %bitcast.31), custom_call_target="tpu_custom_call" | custom-call | tf_op jit(solution)/shard_map/pallas_call | solution.py:333
  118.6 1.0 reshape.158
  119.6 0.2 fusion
  119.8 12.6 %shard_map.254 = (f32[4,2,288,256]{3,2,1,0:T(8,128)S(1)}, f32[4,2,256,512]{3,2,1,0:T(8,128)}, f32[4,2,128,256]{3,2,1,0:T(8,128)S(1)}) custom-call(f32[16,128]{1,0:T(8,128)S(1)} %reshape.159.coeff_ref, f32[45,32,128]{2,1,0:T(8,128)S(1)} %reshape.156.basis_ref, f32[128,128]{1,0:T(8,128)S(1)} %copy-done.15, bf16[256,512]{1,0:T(8,128)(2,1)S(1)} %copy-done.6, ...), custom_call_target="tpu_custom_call" | custom-call | flops 10000000000 | bytes 8388608 | tf_op jit(solution)/shard_map/pallas_call | solution.py:423
  132.4 1.5 copy-done.25
  133.9 14.2 %shard_map.255 = f32[4,4,128]{2,1,0:T(4,128)S(1)} custom-call(f32[4,2,288,256]{3,2,1,0:T(8,128)S(1)} %copy-done.24, f32[4,2,288,256]{3,2,1,0:T(8,128)} %copy-done.25, f32[4,2,256,512]{3,2,1,0:T(8,128)} %get-tuple-element.48.field_ref, f32[4,2,128,256]{3,2,1,0:T(8,128)S(1)} %get-tuple-element.49.pupil_ref, f32[45,32,128]{2,1,0:T(8,128)S(1)} %reshape.156.basis_ref, ...), custom_call_target="tpu_custom_call" | custom-call | flops 10000000000 | bytes 8388608 | tf_op jit(solution)/shard_map/pallas_call | solution.py:433
  148.1 0.6 copy-done.1
  148.7 13.3 %shard_map.256 = f32[32,16,128]{2,1,0:T(8,128)} custom-call(f32[16,128]{1,0:T(8,128)} %bitcast.30), custom_call_target="tpu_custom_call" | custom-call | tf_op jit(solution)/shard_map/pallas_call | solution.py:333
  161.9 1.0 reshape.161
  162.9 0.2 fusion.4
  163.1 0.6 fusion.12
  (71 shorter events, 0.9 us)
Async XLA Ops:
  17.2 1.6 copy-start
  31.1 6.1 %copy-start.30 = (f32[32,8,128]{2,1,0:T(8,128)S(1)}, f32[32,8,128]{2,1,0:T(8,128)}, u32[]{:S(2)}) copy-start(f32[32,8,128]{2,1,0:T(8,128)} %shard_map.248) | copy-start | bytes 393220
  31.1 6.3 %copy-start.32 = (s32[4]{0:T(128)S(1)}, s32[4]{0:T(128)}, u32[]{:S(2)}) copy-start(s32[4]{0:T(128)} %param.33) | copy-start | bytes 52
  31.1 6.4 %slice-start = ((f32[32,8,128]{2,1,0:T(8,128)}), f32[32,4,128]{2,1,0:T(4,128)S(1)}, s32[]{:S(2)}) async-start(f32[32,8,128]{2,1,0:T(8,128)} %shard_map.248), calls=%async_computation.1 | async-start | bytes 131072 | tf_op jit(solution)/shard_map/slice | solution.py:369
  31.1 6.6 %copy-start.29 = (f32[45,4096]{1,0:T(8,128)S(1)}, f32[45,4096]{1,0:T(8,128)}, u32[]{:S(2)}) copy-start(f32[45,4096]{1,0:T(8,128)} %param.35) | copy-start | bytes 2211844
  31.1 54.9 %all-to-all-start = ((f32[32,128,128]{2,1,0:T(8,128)}), f32[32,128,128]{2,1,0:T(8,128)}, u32[]{:S(2)}, u32[]{:S(2)}) async-start(f32[32,128,128]{2,1,0:T(8,128)} %shard_map.249), calls=%async_computation | async-start | bytes 4194304 | tf_op jit(solution)/shard_map/all_to_all | solution.py:387
  39.4 3.6 %copy-start.5 = (bf16[256,512]{1,0:T(8,128)(2,1)S(1)}, bf16[256,512]{1,0:T(8,128)(2,1)}, u32[]{:S(2)}) copy-start(bf16[256,512]{1,0:T(8,128)(2,1)} %constant.154.clone.right_low) | copy-start | bytes 786436
  39.4 3.6 %copy-start.6 = (bf16[256,512]{1,0:T(8,128)(2,1)S(1)}, bf16[256,512]{1,0:T(8,128)(2,1)}, u32[]{:S(2)}) copy-start(bf16[256,512]{1,0:T(8,128)(2,1)} %constant.153.clone.right_high) | copy-start | bytes 786436
  39.4 3.6 %copy-start.7 = (bf16[256,256]{1,0:T(8,128)(2,1)S(1)}, bf16[256,256]{1,0:T(8,128)(2,1)}, u32[]{:S(2)}) copy-start(bf16[256,256]{1,0:T(8,128)(2,1)} %constant.166.clone.mixed_low) | copy-start | bytes 393220
  39.4 3.6 %copy-start.8 = (bf16[256,256]{1,0:T(8,128)(2,1)S(1)}, bf16[256,256]{1,0:T(8,128)(2,1)}, u32[]{:S(2)}) copy-start(bf16[256,256]{1,0:T(8,128)(2,1)} %constant.165.clone.mixed_high) | copy-start | bytes 393220
  39.4 3.6 %copy-start.15 = (f32[128,128]{1,0:T(8,128)S(1)}, f32[128,128]{1,0:T(8,128)}, u32[]{:S(2)}) copy-start(f32[128,128]{1,0:T(8,128)} %constant.171.clone.mask_ref) | copy-start | bytes 196612
  39.5 3.6 %copy-start.16 = (bf16[256,128]{1,0:T(8,128)(2,1)S(1)}, bf16[256,128]{1,0:T(8,128)(2,1)}, u32[]{:S(2)}) copy-start(bf16[256,128]{1,0:T(8,128)(2,1)} %constant.158.clone.left_low) | copy-start | bytes 196612
  39.5 3.6 %copy-start.17 = (bf16[256,128]{1,0:T(8,128)(2,1)S(1)}, bf16[256,128]{1,0:T(8,128)(2,1)}, u32[]{:S(2)}) copy-start(bf16[256,128]{1,0:T(8,128)(2,1)} %constant.157.clone.left_high) | copy-start | bytes 196612
  39.5 3.6 %copy-start.19 = (bf16[144,128]{1,0:T(8,128)(2,1)S(1)}, bf16[144,128]{1,0:T(8,128)(2,1)}, u32[]{:S(2)}) copy-start(bf16[144,128]{1,0:T(8,128)(2,1)} %constant.162.clone.rows_low) | copy-start | bytes 110596
  39.5 3.6 %copy-start.20 = (bf16[144,128]{1,0:T(8,128)(2,1)S(1)}, bf16[144,128]{1,0:T(8,128)(2,1)}, u32[]{:S(2)}) copy-start(bf16[144,128]{1,0:T(8,128)(2,1)} %constant.161.clone.rows_high) | copy-start | bytes 110596
  55.8 1.5 copy-start.26
  57.2 1.0 copy-start.27
  86.1 1.9 %copy-start.9 = (bf16[256,256]{1,0:T(8,128)(2,1)S(1)}, bf16[256,256]{1,0:T(8,128)(2,1)}, u32[]{:S(2)}) copy-start(bf16[256,256]{1,0:T(8,128)(2,1)} %constant.170.clone.mixed_low) | copy-start | bytes 393220
  86.1 1.9 %copy-start.10 = (bf16[256,256]{1,0:T(8,128)(2,1)S(1)}, bf16[256,256]{1,0:T(8,128)(2,1)}, u32[]{:S(2)}) copy-start(bf16[256,256]{1,0:T(8,128)(2,1)} %constant.169.clone.mixed_high) | copy-start | bytes 393220
  86.1 1.9 %copy-start.21 = (bf16[144,128]{1,0:T(8,128)(2,1)S(1)}, bf16[144,128]{1,0:T(8,128)(2,1)}, u32[]{:S(2)}) copy-start(bf16[144,128]{1,0:T(8,128)(2,1)} %constant.168.clone.rows_low) | copy-start | bytes 110596
  86.1 2.0 %copy-start.22 = (bf16[144,128]{1,0:T(8,128)(2,1)S(1)}, bf16[144,128]{1,0:T(8,128)(2,1)}, u32[]{:S(2)}) copy-start(bf16[144,128]{1,0:T(8,128)(2,1)} %constant.167.clone.rows_high) | copy-start | bytes 110596
  88.0 4.6 %copy-start.3 = (bf16[512,256]{1,0:T(8,128)(2,1)S(1)}, bf16[512,256]{1,0:T(8,128)(2,1)}, u32[]{:S(2)}) copy-start(bf16[512,256]{1,0:T(8,128)(2,1)} %constant.156.clone.right_low) | copy-start | bytes 786436
  88.1 4.5 %copy-start.4 = (bf16[512,256]{1,0:T(8,128)(2,1)S(1)}, bf16[512,256]{1,0:T(8,128)(2,1)}, u32[]{:S(2)}) copy-start(bf16[512,256]{1,0:T(8,128)(2,1)} %constant.155.clone.right_high) | copy-start | bytes 786436
  88.1 4.5 %copy-start.11 = (bf16[128,144]{1,0:T(8,128)(2,1)S(1)}, bf16[128,144]{1,0:T(8,128)(2,1)}, u32[]{:S(2)}) copy-start(bf16[128,144]{1,0:T(8,128)(2,1)} %constant.164.clone.rows_low) | copy-start | bytes 110596
  88.1 4.5 %copy-start.12 = (bf16[128,144]{1,0:T(8,128)(2,1)S(1)}, bf16[128,144]{1,0:T(8,128)(2,1)}, u32[]{:S(2)}) copy-start(bf16[128,144]{1,0:T(8,128)(2,1)} %constant.163.clone.rows_high) | copy-start | bytes 110596
  88.1 4.5 %copy-start.13 = (bf16[128,256]{1,0:T(8,128)(2,1)S(1)}, bf16[128,256]{1,0:T(8,128)(2,1)}, u32[]{:S(2)}) copy-start(bf16[128,256]{1,0:T(8,128)(2,1)} %constant.160.clone.left_low) | copy-start | bytes 196612
  88.1 4.5 %copy-start.14 = (bf16[128,256]{1,0:T(8,128)(2,1)S(1)}, bf16[128,256]{1,0:T(8,128)(2,1)}, u32[]{:S(2)}) copy-start(bf16[128,256]{1,0:T(8,128)(2,1)} %constant.159.clone.left_high) | copy-start | bytes 196612
  88.1 4.5 %copy-start.18 = (f32[72,128]{1,0:T(8,128)S(1)}, f32[72,128]{1,0:T(8,128)}, u32[]{:S(2)}) copy-start(f32[72,128]{1,0:T(8,128)} %constant.172.clone.weight_ref) | copy-start | bytes 110596
  88.1 4.5 %copy-start.28 = (f32[4,2,128,256]{3,2,1,0:T(8,128)S(1)}, f32[4,2,128,256]{3,2,1,0:T(8,128)}, u32[]{:S(2)}) copy-start(f32[4,2,128,256]{3,2,1,0:T(8,128)} %copy-done.27) | copy-start | bytes 3145732
  92.6 14.9 %copy-start.23 = (f32[4,2,288,256]{3,2,1,0:T(8,128)}, f32[4,2,288,256]{3,2,1,0:T(8,128)S(1)}, u32[]{:S(2)}) copy-start(f32[4,2,288,256]{3,2,1,0:T(8,128)S(1)} %shard_map.250.data_ref) | copy-start | bytes 7077892
  119.8 14.1 %copy-start.24 = (f32[4,2,288,256]{3,2,1,0:T(8,128)S(1)}, f32[4,2,288,256]{3,2,1,0:T(8,128)}, u32[]{:S(2)}) copy-start(f32[4,2,288,256]{3,2,1,0:T(8,128)} %copy-done.23) | copy-start | bytes 7077892
  132.4 1.5 copy-start.25
  (3 other events, 1.8 us)

commit v2 on v1

--- a/solution.py
+++ b/solution.py
@@ -45,6 +45,7 @@
         right[1, half, :, half, 1] = cos[:PUP]
     right = right.reshape(2 * SUB, 4 * SUB)
     left = np.block([[cos[:, :PUP], sin[:, :PUP]], [-sin[:, :PUP], cos[:, :PUP]]])
+    left = left.reshape(2 * SUB, 2, PUP // 2, 2).transpose(0, 1, 3, 2).reshape(2 * SUB, SUB)
     rows_cos, rows_sin = np.zeros((HALF, SUB)), np.zeros((HALF, SUB))
     rows_cos[:65], rows_sin[:65] = cos[:65], sin[:65]
     rows = np.concatenate([rows_cos, rows_sin], 0)
@@ -55,7 +56,7 @@
     centred = np.arange(PUP) - PUP / 2 + 0.5
     mask = (centred[:, None] ** 2 + centred[None, :] ** 2 <= (PUP / 2) ** 2).astype(np.float32)
     area = float(mask.sum())
-    mask = mask.reshape(2, PUP // 2, PUP).transpose(1, 0, 2).reshape(PUP // 2, SUB)
+    mask = mask.reshape(PUP // 2, SUB)
     return {
         "right": right,
         "right_t": right.T,
@@ -130,21 +131,25 @@
     return const_right(stacked, mixed_high, mixed_low)
 
 
-def window_kernel(anchor_ref, image_ref, out_ref):
-    anchor = anchor_ref[pl.program_id(0)]
+def window_kernel(batch, anchor_ref, image_ref, out_ref):
     last = image_ref.shape[1] - SUB
-    base = pl.multiple_of((anchor // SUB) * SUB, SUB)
-    after = pl.multiple_of(jnp.minimum(base + SUB, last), SUB)
-    shift = anchor - base
-    first = image_ref[:, pl.ds(base, SUB)]
-    second = image_ref[:, pl.ds(after, SUB)]
-    second = jnp.where(base + SUB <= last, second, 0.0)
-    both = jnp.concatenate([first, second], 1)
-    out_ref[0] = pltpu.roll(both, 2 * SUB - shift, 1)[:, :SUB]
+    lane = lax.broadcasted_iota(jnp.int32, (image_ref.shape[0], SUB), 1)
+    for k in range(batch):
+        anchor = anchor_ref[pl.program_id(0) * batch + k]
+        base = pl.multiple_of((anchor // SUB) * SUB, SUB)
+        after = pl.multiple_of(jnp.minimum(base + SUB, last), SUB)
+        shift = anchor - base
+        turn = lax.rem(SUB - shift, SUB)
+        first = pltpu.roll(image_ref[:, pl.ds(base, SUB)], turn, 1)
+        second = pltpu.roll(image_ref[:, pl.ds(after, SUB)], turn, 1)
+        reach = jnp.where(base + SUB <= last, SUB, 0)
+        out_ref[k] = jnp.where(
+            lane < SUB - shift, first, jnp.where(lane < reach, second, 0.0)
+        )
 
 
 def data_kernel(cells_ref, rows_high, rows_low, mixed_high, mixed_low, out_ref):
-    images = jnp.concatenate([cells_ref[0, f] for f in range(FRAMES)], 1)
+    images = jnp.concatenate([cells_ref[:, 0, 0, f].reshape(SUB, SUB) for f in range(FRAMES)], 1)
     out_ref[0, 0] = half_plane(images, rows_high, rows_low, mixed_high, mixed_low)
 
 
@@ -363,30 +368,43 @@
     tile_rows = -(-(owned_rows + 2) // 8) * 8
     mine = jnp.zeros((tile_rows, SUB), F32)
     mine = mine.at[:owned_rows, :modes].set(coeffs.transpose(2, 0, 1).reshape(owned_rows, modes))
+    owned_row_patch = owned_rows
     mine = mine.at[owned_rows, :per].set(patches.astype(F32))
     mine = mine.at[owned_rows + 1, :per].set(anchors.astype(F32))
     everyone = spread_blocks(mine, 0)
     all_coeffs = everyone[:, :owned_rows, :].reshape(devices * owned, FRAMES * SUB)
-    all_patches = everyone[:, owned_rows, :per].reshape(devices * per).astype(jnp.int32)
-    tile = (device * rows) // SUB
-    tile_anchors = lax.dynamic_index_in_dim(everyone[:, owned_rows + 1, :], tile, 1, keepdims=False)
-    tile_anchors = tile_anchors.astype(jnp.int32)
-
+    group = devices // TR
+    tile = device // group
+    place = device % group
+    share = devices * per // TR // group
+    all_patches = everyone[:, owned_row_patch, :per].reshape(devices * per // TR, TR)
+    all_anchors = everyone[:, owned_row_patch + 1, :per].reshape(devices * per // TR, TR)
+    all_patches = all_patches.astype(jnp.int32).T
+    pick_tile = (jnp.arange(TR, dtype=jnp.int32) == tile)[None, :]
+    tile_anchors = jnp.sum(jnp.where(pick_tile, all_anchors, 0.0), axis=1).astype(jnp.int32)
+    patches = lax.dynamic_slice(all_patches, (tile, place * share), (1, share)).reshape(share)
+    all_patches = all_patches.reshape(devices * per)
+
+    count = devices * per // TR
+    batch = 8
     bands = images.reshape(CH * FRAMES * rows, images.shape[3])
     windows = pl.pallas_call(
-        window_kernel,
+        functools.partial(window_kernel, batch),
         grid_spec=pltpu.PrefetchScalarGridSpec(
             num_scalar_prefetch=1,
-            grid=(devices,),
+            grid=(count // batch,),
             in_specs=[pl.BlockSpec(bands.shape, lambda j, a: (0, 0), pipeline_mode=pl.Buffered(1))],
-            out_specs=pl.BlockSpec((1, bands.shape[0], SUB), lambda j, a: (j, 0, 0)),
+            out_specs=pl.BlockSpec((batch, bands.shape[0], SUB), lambda j, a: (j, 0, 0)),
         ),
-        out_shape=jax.ShapeDtypeStruct((devices, bands.shape[0], SUB), F32),
+        out_shape=jax.ShapeDtypeStruct((count, bands.shape[0], SUB), F32),
         compiler_params=pltpu.CompilerParams(vmem_limit_bytes=VMEM_LIMIT),
     )(tile_anchors, bands)
-    received = lax.all_to_all(windows, "sub", 0, 0, tiled=True)
-    cells = received.reshape(TR, devices // TR, CH * FRAMES, rows, SUB)
-    cells = cells.transpose(0, 2, 1, 3, 4).reshape(TR, CH * FRAMES, SUB, SUB)
+    teams = [list(range(g * group, (g + 1) * group)) for g in range(TR)]
+    received = lax.all_to_all(windows, "sub", 0, 0, axis_index_groups=teams, tiled=True)
+    cells = received.reshape(group, share, CH, FRAMES, rows, SUB)
+    if rows % 8:
+        cells = cells.transpose(1, 2, 3, 0, 4, 5).reshape(1, share, CH, FRAMES, SUB, SUB)
+    per = share
 
     big = pltpu.CompilerParams(vmem_limit_bytes=VMEM_LIMIT)
     spectrum_shape = jax.ShapeDtypeStruct((per, CH, FRAMES * HALF, 2 * SUB), F32)
@@ -398,7 +416,11 @@
     data = pl.pallas_call(
         data_kernel,
         grid=(per, CH),
-        in_specs=[pl.BlockSpec((1, FRAMES, SUB, SUB), lambda s, c: (s, c, 0, 0))]
+        in_specs=[
+            pl.BlockSpec(
+                (cells.shape[0], 1, 1) + cells.shape[3:], lambda s, c: (0, s, c, 0, 0, 0)
+            )
+        ]
         + [whole(t) for t in data_tables],
         out_specs=per_block(FRAMES * HALF, 2 * SUB),
         out_shape=spectrum_shape,
@@ -406,7 +428,7 @@
         cost_estimate=pl.CostEstimate(flops=6 * 10**9, bytes_accessed=5 << 20, transcendentals=0),
     )(cells, *data_tables)
 
-    basis = zbasis.reshape(modes, 2, PUP // 2, PUP).transpose(0, 2, 1, 3).reshape(modes, PUP // 2, SUB)
+    basis = zbasis.reshape(modes, PUP // 2, SUB)
     mask = jnp.asarray(tables["mask"])
     weight = jnp.asarray(tables["weight"])
     forward_tables = pairs["right"] + pairs["left"] + pairs["rows"] + pairs["mixed"]

time: 164 us -> 134 us (0.82)
  waiting for transfers between devices: 27.9 us -> 4.56 us
  Pallas kernels: 107 us -> 98.6 us
  local copies, waits for them, and re-layouts: 18.6 us -> 20.3 us
    all_to_all x1, waiting for transfers between devices: 27.9 us -> 4.56 us  [on_device(): lax.all_to_all(windows, 'sub', 0, 0, axis_index_groups=teams, tiled=True)]
    pallas_call x2, Pallas kernels: 16.8 us -> 7.89 us  [the longest x1 4.65 us: on_device(): pl.pallas_call(data_kernel, grid=(per, CH), in_specs=[pl.BlockSpec((cells...]
    unnamed x66 -> x89, local copies, waits for them, and re-layouts: 7.43 us -> 16.3 us
    reshape x4 -> x1, local copies, waits for them, and re-layouts: 7.17 us -> 0.05 us  [on_device(): basis = zbasis.reshape(modes, PUP // 2, SUB)]
  transfers between devices with their start and end apart: 1 -> 1, of which waited for: 1 -> 1; matrix products, arithmetic and copies ran while one was open for 3% -> 2% of each run, Pallas kernels for 8% -> 10%
where the time goes in v2:
time: 134 us; the launch traced here: 133 us
  Pallas kernels  98.6 us (74%)
  local copies, waits for them, and re-layouts  20.3 us (15%)
  waiting for transfers between devices  4.56 us (3%)
  starting transfers between devices  4.47 us (3%)
  other arithmetic  3.11 us (2%)
    pallas_call x3, Pallas kernels, spread_blocks(): pl.pallas_call(functools.partial(gather_kernel, n), out_shape=jax.ShapeDt...  35.9 us
    pallas_call x2, Pallas kernels, slopes_of(): pl.pallas_call(functools.partial(backward_kernel, scale), grid=(per, CH),...  29.1 us
    pallas_call x2, Pallas kernels, slopes_of(): pl.pallas_call(functools.partial(forward_kernel, scale, modes), grid=(per...  25.7 us
    unnamed x89, local copies, waits for them, and re-layouts  16.3 us
    pallas_call x1, Pallas kernels, on_device(): pl.pallas_call(data_kernel, grid=(per, CH), in_specs=[pl.BlockSpec((cells...  4.65 us
    all_to_all x1, waiting for transfers between devices, on_device(): lax.all_to_all(windows, 'sub', 0, 0, axis_index_groups=teams, tiled=True)  4.56 us
    all_to_all x1, starting transfers between devices, on_device(): lax.all_to_all(windows, 'sub', 0, 0, axis_index_groups=teams, tiled=True)  4.47 us
    pallas_call x1, Pallas kernels, on_device(): pl.pallas_call(functools.partial(window_kernel, batch), grid_spec=pltpu.P...  3.24 us
  transfers between devices with their start and end apart: 1, of which 1 were waited for; matrix products, arithmetic and copies ran while one was open for 2% of the time, Pallas kernels for 10%

profile of v2, /device:TPU:0, one launch (start us, length us, event | category | flops | bytes accessed | tf_op | source)
XLA Modules:
  0.0 132.9 jit_solution(16484792267904698305)
XLA Ops:
  0.7 0.7 convert_bitcast_fusion
  1.3 0.7 convert_bitcast_fusion.1
  2.0 0.7 scatter.10
  3.5 11.9 %shard_map.248 = f32[32,8,128]{2,1,0:T(8,128)} custom-call(f32[8,128]{1,0:T(8,128)} %copy-done.42), custom_call_target="tpu_custom_call" | custom-call | tf_op jit(solution)/shard_map/pallas_call | solution.py:338
  15.5 1.0 fusion.13
  16.7 1.6 %copy-done = f32[2,4,16,4096]{3,2,1,0:T(8,128)S(1)} copy-done((f32[2,4,16,4096]{3,2,1,0:T(8,128)S(1)}, f32[2,4,16,4096]{3,2,1,0:T(8,128)}, u32[]{:S(2)}) %copy-start) | copy-done | bytes 2097176
  18.3 3.2 %shard_map.249 = f32[32,128,128]{2,1,0:T(8,128)} custom-call(s32[32]{0:T(128)S(1)} %convert_element_type.21.anchor_ref, f32[128,4096]{1,0:T(8,128)S(1)} %bitcast.32), custom_call_target="tpu_custom_call" | custom-call | tf_op jit(solution)/shard_map/pallas_call | solution.py:391
  21.5 4.5 %all-to-all-start = ((f32[32,128,128]{2,1,0:T(8,128)}), f32[32,128,128]{2,1,0:T(8,128)S(1)}, u32[]{:S(2)}, u32[]{:S(2)}) async-start(f32[32,128,128]{2,1,0:T(8,128)} %shard_map.249), calls=%async_computation | async-start | bytes 4194304 | tf_op jit(solution)/shard_map/all_to_all | solution.py:403
  27.3 1.3 copy.32
  28.6 0.9 copy-done.10
  29.5 0.8 copy-done.23
  30.4 0.8 copy-done.25
  31.2 0.8 copy-done.27
  32.1 0.8 copy-done.32
  32.8 12.8 %shard_map.251 = (f32[4,2,288,256]{3,2,1,0:T(8,128)S(1)}, f32[4,2,256,512]{3,2,1,0:T(8,128)}, f32[4,2,128,256]{3,2,1,0:T(8,128)S(1)}) custom-call(f32[16,128]{1,0:T(8,128)S(1)} %reshape.152.coeff_ref, f32[45,32,128]{2,1,0:T(8,128)S(1)} %slice.99.basis_ref, f32[128,128]{1,0:T(8,128)S(1)} %copy-done.23, bf16[256,512]{1,0:T(8,128)(2,1)S(1)} %copy-done.7, ...), custom_call_target="tpu_custom_call" | custom-call | flops 10000000000 | bytes 8388608 | tf_op jit(solution)/shard_map/pallas_call | solution.py:445
  45.6 1.5 %copy-done.39 = f32[4,2,288,256]{3,2,1,0:T(8,128)} copy-done((f32[4,2,288,256]{3,2,1,0:T(8,128)}, f32[4,2,288,256]{3,2,1,0:T(8,128)S(1)}, u32[]{:S(2)}) %copy-start.39) | copy-done | bytes 2359320
  47.1 1.0 copy-done.40
  48.1 4.6 %all-to-all-done = f32[32,128,128]{2,1,0:T(8,128)S(1)} async-done(((f32[32,128,128]{2,1,0:T(8,128)}), f32[32,128,128]{2,1,0:T(8,128)S(1)}, u32[]{:S(2)}, u32[]{:S(2)}) %all-to-all-start) | async-done | bytes 2097184 | tf_op jit(solution)/shard_map/all_to_all | solution.py:403
  52.6 0.9 copy-done.13
  53.5 0.9 copy-done.14
  54.4 0.8 copy-done.34
  55.2 0.8 copy-done.35
  56.1 4.7 %shard_map.250.data_ref = f32[4,2,288,256]{3,2,1,0:T(8,128)S(1)} custom-call(f32[8,4,2,4,16,128]{5,4,3,2,1,0:T(8,128)S(1)} %bitcast.33, bf16[144,128]{1,0:T(8,128)(2,1)S(1)} %copy-done.35, bf16[144,128]{1,0:T(8,128)(2,1)S(1)} %copy-done.34, bf16[256,256]{1,0:T(8,128)(2,1)S(1)} %copy-done.14, bf16[256,256]{1,0:T(8,128)(2,1)S(1)} %copy-done.13), custom_call_target="tpu_custom_call" | custom-call | flops 6000000000 | bytes 5242880 | tf_op jit(solution)/shard_map/pallas_call | solution.py:416
  60.9 15.0 %shard_map.252 = f32[4,4,128]{2,1,0:T(4,128)S(1)} custom-call(f32[4,2,288,256]{3,2,1,0:T(8,128)S(1)} %shard_map.250.data_ref, f32[4,2,288,256]{3,2,1,0:T(8,128)} %copy-done.39, f32[4,2,256,512]{3,2,1,0:T(8,128)} %get-tuple-element.45.field_ref, f32[4,2,128,256]{3,2,1,0:T(8,128)S(1)} %copy-done.41, f32[45,32,128]{2,1,0:T(8,128)S(1)} %slice.99.basis_ref, ...), custom_call_target="tpu_custom_call" | custom-call | flops 10000000000 | bytes 8388608 | tf_op jit(solution)/shard_map/pallas_call | solution.py:455
  76.5 11.8 %shard_map.253 = f32[32,16,128]{2,1,0:T(8,128)} custom-call(f32[16,128]{1,0:T(8,128)} %bitcast.35), custom_call_target="tpu_custom_call" | custom-call | tf_op jit(solution)/shard_map/pallas_call | solution.py:338
  88.3 1.0 reshape.155
  89.7 12.9 %shard_map.254 = (f32[4,2,288,256]{3,2,1,0:T(8,128)S(1)}, f32[4,2,256,512]{3,2,1,0:T(8,128)}, f32[4,2,128,256]{3,2,1,0:T(8,128)S(1)}) custom-call(f32[16,128]{1,0:T(8,128)S(1)} %reshape.156.coeff_ref, f32[45,32,128]{2,1,0:T(8,128)S(1)} %slice.99.basis_ref, f32[128,128]{1,0:T(8,128)S(1)} %copy-done.24, bf16[256,512]{1,0:T(8,128)(2,1)S(1)} %copy-done.8, ...), custom_call_target="tpu_custom_call" | custom-call | flops 10000000000 | bytes 8388608 | tf_op jit(solution)/shard_map/pallas_call | solution.py:445
  102.5 1.5 %copy-done.38 = f32[4,2,288,256]{3,2,1,0:T(8,128)} copy-done((f32[4,2,288,256]{3,2,1,0:T(8,128)}, f32[4,2,288,256]{3,2,1,0:T(8,128)S(1)}, u32[]{:S(2)}) %copy-start.38) | copy-done | bytes 2359320
  104.0 14.2 %shard_map.255 = f32[4,4,128]{2,1,0:T(4,128)S(1)} custom-call(f32[4,2,288,256]{3,2,1,0:T(8,128)S(1)} %copy-done.37, f32[4,2,288,256]{3,2,1,0:T(8,128)} %copy-done.38, f32[4,2,256,512]{3,2,1,0:T(8,128)} %get-tuple-element.48.field_ref, f32[4,2,128,256]{3,2,1,0:T(8,128)S(1)} %get-tuple-element.49.pupil_ref, f32[45,32,128]{2,1,0:T(8,128)S(1)} %slice.99.basis_ref, ...), custom_call_target="tpu_custom_call" | custom-call | flops 10000000000 | bytes 8388608 | tf_op jit(solution)/shard_map/pallas_call | solution.py:455
  118.2 0.6 copy-done.1
  118.8 12.2 %shard_map.256 = f32[32,16,128]{2,1,0:T(8,128)} custom-call(f32[16,128]{1,0:T(8,128)} %bitcast.34), custom_call_target="tpu_custom_call" | custom-call | tf_op jit(solution)/shard_map/pallas_call | solution.py:338
  131.1 1.0 reshape.158
  (95 shorter events, 4.1 us)
Async XLA Ops:
  16.7 1.6 %copy-start = (f32[2,4,16,4096]{3,2,1,0:T(8,128)S(1)}, f32[2,4,16,4096]{3,2,1,0:T(8,128)}, u32[]{:S(2)}) copy-start(f32[2,4,16,4096]{3,2,1,0:T(8,128)} %param.31) | copy-start | bytes 6291460
  21.5 5.5 %slice-start = ((f32[32,8,128]{2,1,0:T(8,128)}), f32[32,4,128]{2,1,0:T(4,128)S(1)}, s32[]{:S(2)}) async-start(f32[32,8,128]{2,1,0:T(8,128)} %shard_map.248), calls=%async_computation.1 | async-start | bytes 131072 | tf_op jit(solution)/shard_map/slice | solution.py:375
  21.5 31.1 %all-to-all-start = ((f32[32,128,128]{2,1,0:T(8,128)}), f32[32,128,128]{2,1,0:T(8,128)S(1)}, u32[]{:S(2)}, u32[]{:S(2)}) async-start(f32[32,128,128]{2,1,0:T(8,128)} %shard_map.249), calls=%async_computation | async-start | bytes 4194304 | tf_op jit(solution)/shard_map/all_to_all | solution.py:403
  26.0 2.6 %copy-start.5 = (bf16[256,512]{1,0:T(8,128)(2,1)S(1)}, bf16[256,512]{1,0:T(8,128)(2,1)}, u32[]{:S(2)}) copy-start(bf16[256,512]{1,0:T(8,128)(2,1)} %constant.162.clone.right_low) | copy-start | bytes 786436
  26.0 2.6 %copy-start.7 = (bf16[256,512]{1,0:T(8,128)(2,1)S(1)}, bf16[256,512]{1,0:T(8,128)(2,1)}, u32[]{:S(2)}) copy-start(bf16[256,512]{1,0:T(8,128)(2,1)} %constant.161.clone.right_high) | copy-start | bytes 786436
  26.0 2.6 %copy-start.9 = (bf16[256,256]{1,0:T(8,128)(2,1)S(1)}, bf16[256,256]{1,0:T(8,128)(2,1)}, u32[]{:S(2)}) copy-start(bf16[256,256]{1,0:T(8,128)(2,1)} %constant.174.clone.mixed_low) | copy-start | bytes 393220
  26.0 2.6 %copy-start.30 = (bf16[144,128]{1,0:T(8,128)(2,1)S(1)}, bf16[144,128]{1,0:T(8,128)(2,1)}, u32[]{:S(2)}) copy-start(bf16[144,128]{1,0:T(8,128)(2,1)} %constant.170.clone.rows_low) | copy-start | bytes 110596
  45.6 1.5 %copy-start.39 = (f32[4,2,288,256]{3,2,1,0:T(8,128)}, f32[4,2,288,256]{3,2,1,0:T(8,128)S(1)}, u32[]{:S(2)}) copy-start(f32[4,2,288,256]{3,2,1,0:T(8,128)S(1)} %get-tuple-element.44.otf_ref) | copy-start | bytes 7077892
  56.0 4.7 %copy-start.3 = (bf16[512,256]{1,0:T(8,128)(2,1)S(1)}, bf16[512,256]{1,0:T(8,128)(2,1)}, u32[]{:S(2)}) copy-start(bf16[512,256]{1,0:T(8,128)(2,1)} %constant.164.clone.right_low) | copy-start | bytes 786436
  56.0 4.8 %copy-start.4 = (bf16[512,256]{1,0:T(8,128)(2,1)S(1)}, bf16[512,256]{1,0:T(8,128)(2,1)}, u32[]{:S(2)}) copy-start(bf16[512,256]{1,0:T(8,128)(2,1)} %constant.163.clone.right_high) | copy-start | bytes 786436
  56.0 4.8 %copy-start.11 = (bf16[256,256]{1,0:T(8,128)(2,1)S(1)}, bf16[256,256]{1,0:T(8,128)(2,1)}, u32[]{:S(2)}) copy-start(bf16[256,256]{1,0:T(8,128)(2,1)} %constant.173.clone.mixed_high) | copy-start | bytes 393220
  56.0 4.8 %copy-start.15 = (bf16[128,144]{1,0:T(8,128)(2,1)S(1)}, bf16[128,144]{1,0:T(8,128)(2,1)}, u32[]{:S(2)}) copy-start(bf16[128,144]{1,0:T(8,128)(2,1)} %constant.172.clone.rows_low) | copy-start | bytes 110596
  56.0 4.8 %copy-start.17 = (bf16[128,144]{1,0:T(8,128)(2,1)S(1)}, bf16[128,144]{1,0:T(8,128)(2,1)}, u32[]{:S(2)}) copy-start(bf16[128,144]{1,0:T(8,128)(2,1)} %constant.171.clone.rows_high) | copy-start | bytes 110596
  56.0 4.8 %copy-start.19 = (bf16[128,256]{1,0:T(8,128)(2,1)S(1)}, bf16[128,256]{1,0:T(8,128)(2,1)}, u32[]{:S(2)}) copy-start(bf16[128,256]{1,0:T(8,128)(2,1)} %constant.168.clone.left_low) | copy-start | bytes 196612
  56.0 4.8 %copy-start.21 = (bf16[128,256]{1,0:T(8,128)(2,1)S(1)}, bf16[128,256]{1,0:T(8,128)(2,1)}, u32[]{:S(2)}) copy-start(bf16[128,256]{1,0:T(8,128)(2,1)} %constant.167.clone.left_high) | copy-start | bytes 196612
  56.0 4.8 %copy-start.29 = (f32[72,128]{1,0:T(8,128)S(1)}, f32[72,128]{1,0:T(8,128)}, u32[]{:S(2)}) copy-start(f32[72,128]{1,0:T(8,128)} %constant.180.clone.weight_ref) | copy-start | bytes 110596
  56.0 4.8 %copy-start.41 = (f32[4,2,128,256]{3,2,1,0:T(8,128)S(1)}, f32[4,2,128,256]{3,2,1,0:T(8,128)}, u32[]{:S(2)}) copy-start(f32[4,2,128,256]{3,2,1,0:T(8,128)} %copy-done.40) | copy-start | bytes 3145732
  60.7 15.2 %copy-start.36 = (f32[4,2,288,256]{3,2,1,0:T(8,128)}, f32[4,2,288,256]{3,2,1,0:T(8,128)S(1)}, u32[]{:S(2)}) copy-start(f32[4,2,288,256]{3,2,1,0:T(8,128)S(1)} %shard_map.250.data_ref) | copy-start | bytes 7077892
  60.8 28.5 %copy-start.43 = (s32[128]{0:T(128)S(1)}, s32[128]{0:T(128)}, u32[]{:S(2)}) copy-start(s32[128]{0:T(128)} %eq.44) | copy-start | bytes 1540
  60.8 28.7 %copy-start.6 = (bf16[256,512]{1,0:T(8,128)(2,1)S(1)}, bf16[256,512]{1,0:T(8,128)(2,1)}, u32[]{:S(2)}) copy-start(bf16[256,512]{1,0:T(8,128)(2,1)} %constant.162.clone.right_low) | copy-start | bytes 786436
  60.8 28.7 %copy-start.8 = (bf16[256,512]{1,0:T(8,128)(2,1)S(1)}, bf16[256,512]{1,0:T(8,128)(2,1)}, u32[]{:S(2)}) copy-start(bf16[256,512]{1,0:T(8,128)(2,1)} %constant.161.clone.right_high) | copy-start | bytes 786436
  60.8 28.7 %copy-start.12 = (bf16[256,256]{1,0:T(8,128)(2,1)S(1)}, bf16[256,256]{1,0:T(8,128)(2,1)}, u32[]{:S(2)}) copy-start(bf16[256,256]{1,0:T(8,128)(2,1)} %constant.173.clone.mixed_high) | copy-start | bytes 393220
  60.9 28.7 %copy-start.24 = (f32[128,128]{1,0:T(8,128)S(1)}, f32[128,128]{1,0:T(8,128)}, u32[]{:S(2)}) copy-start(f32[128,128]{1,0:T(8,128)} %constant.179.clone.mask_ref) | copy-start | bytes 196612
  60.9 28.7 %copy-start.26 = (bf16[256,128]{1,0:T(8,128)(2,1)S(1)}, bf16[256,128]{1,0:T(8,128)(2,1)}, u32[]{:S(2)}) copy-start(bf16[256,128]{1,0:T(8,128)(2,1)} %constant.166.clone.left_low) | copy-start | bytes 196612
  60.9 28.7 %copy-start.28 = (bf16[256,128]{1,0:T(8,128)(2,1)S(1)}, bf16[256,128]{1,0:T(8,128)(2,1)}, u32[]{:S(2)}) copy-start(bf16[256,128]{1,0:T(8,128)(2,1)} %constant.165.clone.left_high) | copy-start | bytes 196612
  60.9 28.7 %copy-start.31 = (bf16[144,128]{1,0:T(8,128)(2,1)S(1)}, bf16[144,128]{1,0:T(8,128)(2,1)}, u32[]{:S(2)}) copy-start(bf16[144,128]{1,0:T(8,128)(2,1)} %constant.170.clone.rows_low) | copy-start | bytes 110596
  60.9 28.7 %copy-start.33 = (bf16[144,128]{1,0:T(8,128)(2,1)S(1)}, bf16[144,128]{1,0:T(8,128)(2,1)}, u32[]{:S(2)}) copy-start(bf16[144,128]{1,0:T(8,128)(2,1)} %constant.169.clone.rows_high) | copy-start | bytes 110596
  89.6 14.4 %copy-start.16 = (bf16[128,144]{1,0:T(8,128)(2,1)S(1)}, bf16[128,144]{1,0:T(8,128)(2,1)}, u32[]{:S(2)}) copy-start(bf16[128,144]{1,0:T(8,128)(2,1)} %constant.172.clone.rows_low) | copy-start | bytes 110596
  89.6 14.4 %copy-start.18 = (bf16[128,144]{1,0:T(8,128)(2,1)S(1)}, bf16[128,144]{1,0:T(8,128)(2,1)}, u32[]{:S(2)}) copy-start(bf16[128,144]{1,0:T(8,128)(2,1)} %constant.171.clone.rows_high) | copy-start | bytes 110596
  89.6 14.4 %copy-start.20 = (bf16[128,256]{1,0:T(8,128)(2,1)S(1)}, bf16[128,256]{1,0:T(8,128)(2,1)}, u32[]{:S(2)}) copy-start(bf16[128,256]{1,0:T(8,128)(2,1)} %constant.168.clone.left_low) | copy-start | bytes 196612
  89.7 14.4 %copy-start.22 = (bf16[128,256]{1,0:T(8,128)(2,1)S(1)}, bf16[128,256]{1,0:T(8,128)(2,1)}, u32[]{:S(2)}) copy-start(bf16[128,256]{1,0:T(8,128)(2,1)} %constant.167.clone.left_high) | copy-start | bytes 196612
  89.7 14.4 %copy-start.37 = (f32[4,2,288,256]{3,2,1,0:T(8,128)S(1)}, f32[4,2,288,256]{3,2,1,0:T(8,128)}, u32[]{:S(2)}) copy-start(f32[4,2,288,256]{3,2,1,0:T(8,128)} %copy-done.36) | copy-start | bytes 7077892
  (14 other events, 11.8 us)

commit v3 on v2

--- a/solution.py
+++ b/solution.py
@@ -13,6 +13,8 @@
 SUB = 128
 CH = 2
 FRAMES = 4
+FIELDS = CH * FRAMES
+SLOT = 64
 TR = 4
 ITERS = 2
 PUP = 64
@@ -68,7 +70,7 @@
         "data_rows": rows * taper[None, :],
         "data_mixed": np.concatenate([taper, taper])[:, None] * mixed,
         "weight": np.broadcast_to(weight, (HALF, SUB)).astype(np.float32) * np.float32(-2.0 / SUB**4),
-        "mask": np.tile(mask, (FRAMES, 1)),
+        "mask": np.tile(mask, (FIELDS, 1)),
         "area": area,
     }
 
@@ -117,14 +119,19 @@
     return out_sin, out_cos
 
 
-def half_plane(images, rows_high, rows_low, mixed_high, mixed_low):
-    columns = const_left(rows_high, rows_low, images)
+def stacked_left(twice_ref, low_ref, value):
+    high, low = split(value)
+    return dot(twice_ref[...], jnp.concatenate([high, low], 0)) + dot(low_ref[...], high)
+
+
+def half_plane(images, rows_twice, rows_low, mixed_high, mixed_low):
+    columns = stacked_left(rows_twice, rows_low, images)
     stacked = jnp.concatenate(
         [
             jnp.concatenate(
                 [columns[:HALF, f * SUB : (f + 1) * SUB], columns[HALF:, f * SUB : (f + 1) * SUB]], 1
             )
-            for f in range(FRAMES)
+            for f in range(FIELDS)
         ],
         0,
     )
@@ -148,117 +155,74 @@
         )
 
 
-def data_kernel(cells_ref, rows_high, rows_low, mixed_high, mixed_low, out_ref):
-    images = jnp.concatenate([cells_ref[:, 0, 0, f].reshape(SUB, SUB) for f in range(FRAMES)], 1)
-    out_ref[0, 0] = half_plane(images, rows_high, rows_low, mixed_high, mixed_low)
-
-
-def forward_kernel(
-    scale,
-    modes,
-    coeff_ref,
-    basis_ref,
-    mask_ref,
-    right_high,
-    right_low,
-    left_high,
-    left_low,
-    rows_high,
-    rows_low,
-    mixed_high,
-    mixed_low,
-    otf_ref,
-    field_ref,
-    pupil_ref,
-):
+def forward_math(scale, modes, coeff_ref, basis_ref, mask_ref, tables):
+    right_high, right_low, left_twice, left_low, rows_twice, rows_low, mixed_high, mixed_low = tables
     subfield = pl.program_id(0)
-    channel = pl.program_id(1)
-    ratio = 1.0 / (1.0 + 0.25 * channel.astype(F32))
-    sums = [jnp.zeros((PUP // 2, SUB), F32) for _ in range(FRAMES)]
+    q = PUP // 2
+    sums = [jnp.zeros((q, SUB), F32) for _ in range(FRAMES)]
     for m in range(modes):
         mode = basis_ref[m]
         for f in range(FRAMES):
-            sums[f] = sums[f] + coeff_ref[subfield * FRAMES + f, m] * mode
-    phase = jnp.concatenate(sums, 0) * ratio
+            value = coeff_ref[subfield * 2 + f // 2, (f % 2) * SLOT + m]
+            sums[f] = sums[f] + value * mode
+    phase = jnp.concatenate(sums, 0)
+    phase = jnp.concatenate([phase * np.float32(1.0 / (1.0 + 0.25 * c)) for c in range(CH)], 0)
     sine, cosine = sin_cos(phase)
     mask = mask_ref[...]
     pupil = jnp.concatenate([mask * cosine, mask * sine], 1)
-    pupil_ref[0, 0] = pupil
     half = const_right(pupil, right_high, right_low)
-    q = PUP // 2
     blocks = jnp.concatenate(
         [
             jnp.concatenate(
                 [half[f * q : (f + 1) * q, n * SUB : (n + 1) * SUB] for n in (0, 2, 1, 3)], 0
             )
-            for f in range(FRAMES)
+            for f in range(FIELDS)
         ],
         1,
     )
-    field = const_left(left_high, left_low, blocks)
-    field_ref[0, 0] = field
+    field = stacked_left(left_twice, left_low, blocks)
     psf = (field[:SUB] * field[:SUB] + field[SUB:] * field[SUB:]) * scale
-    otf_ref[0, 0] = half_plane(psf, rows_high, rows_low, mixed_high, mixed_low)
-
-
-def backward_kernel(
-    scale,
-    data_ref,
-    otf_ref,
-    field_ref,
-    pupil_ref,
-    basis_ref,
-    weight_ref,
-    mixed_high,
-    mixed_low,
-    rows_high,
-    rows_low,
-    left_high,
-    left_low,
-    right_high,
-    right_low,
-    out_ref,
-    phase_acc,
-):
-    channel = pl.program_id(1)
-    ratio = 1.0 / (1.0 + 0.25 * channel.astype(F32))
-    data = [data_ref[0, 0, f * HALF : (f + 1) * HALF, :] for f in range(FRAMES)]
-    otf = [otf_ref[0, 0, f * HALF : (f + 1) * HALF, :] for f in range(FRAMES)]
-    cross_real = cross_imag = power = None
-    for f in range(FRAMES):
-        dr, di = data[f][:, :SUB], data[f][:, SUB:]
-        orr, oi = otf[f][:, :SUB], otf[f][:, SUB:]
-        terms = (dr * orr + di * oi, di * orr - dr * oi, orr * orr + oi * oi)
-        if f == 0:
-            cross_real, cross_imag, power = terms
-        else:
-            cross_real = cross_real + terms[0]
-            cross_imag = cross_imag + terms[1]
-            power = power + terms[2]
-    inverse = 1.0 / (power + GAMMA)
-    slope = weight_ref[...] * inverse
-    xr, xi = cross_real * inverse, cross_imag * inverse
-    share = weight_ref[...] * (xr * xr + xi * xi)
-    cross_real, cross_imag = cross_real * slope, cross_imag * slope
+    return half_plane(psf, rows_twice, rows_low, mixed_high, mixed_low), field, pupil
+
+
+def backward_math(scale, data, otf, field, pupil, basis_ref, weight_ref, tables):
+    mixed_high, mixed_low, rows_high, rows_low, left_high, left_low, right_high, right_low = tables
+    weight = weight_ref[...]
     bars = []
-    for f in range(FRAMES):
-        dr, di = data[f][:, :SUB], data[f][:, SUB:]
-        orr, oi = otf[f][:, :SUB], otf[f][:, SUB:]
-        bar_real = cross_real * dr + cross_imag * di - share * orr
-        bar_imag = cross_real * di - cross_imag * dr - share * oi
-        bars.append(jnp.concatenate([bar_real, bar_imag], 1))
+    for c in range(CH):
+        parts = []
+        cross_real = cross_imag = power = None
+        for f in range(c * FRAMES, (c + 1) * FRAMES):
+            d, o = data[f * HALF : (f + 1) * HALF], otf[f * HALF : (f + 1) * HALF]
+            dr, di, orr, oi = d[:, :SUB], d[:, SUB:], o[:, :SUB], o[:, SUB:]
+            parts.append((dr, di, orr, oi))
+            terms = (dr * orr + di * oi, di * orr - dr * oi, orr * orr + oi * oi)
+            if cross_real is None:
+                cross_real, cross_imag, power = terms
+            else:
+                cross_real = cross_real + terms[0]
+                cross_imag = cross_imag + terms[1]
+                power = power + terms[2]
+        inverse = 1.0 / (power + GAMMA)
+        slope = weight * inverse
+        xr, xi = cross_real * inverse, cross_imag * inverse
+        share = weight * (xr * xr + xi * xi)
+        cross_real, cross_imag = cross_real * slope, cross_imag * slope
+        for dr, di, orr, oi in parts:
+            bar_real = cross_real * dr + cross_imag * di - share * orr
+            bar_imag = cross_real * di - cross_imag * dr - share * oi
+            bars.append(jnp.concatenate([bar_real, bar_imag], 1))
     columns = const_right(jnp.concatenate(bars, 0), mixed_high, mixed_low)
     stacked = jnp.concatenate(
         [
             jnp.concatenate(
                 [columns[f * HALF : (f + 1) * HALF, :SUB], columns[f * HALF : (f + 1) * HALF, SUB:]], 0
             )
-            for f in range(FRAMES)
+            for f in range(FIELDS)
         ],
         1,
     )
     psf_bar = const_left(rows_high, rows_low, stacked) * (2.0 * scale)
-    field = field_ref[0, 0]
     field_bar = jnp.concatenate([field[:SUB] * psf_bar, field[SUB:] * psf_bar], 0)
     half_bar = const_left(left_high, left_low, field_bar)
     q = PUP // 2
@@ -267,31 +231,57 @@
             jnp.concatenate(
                 [half_bar[n * q : (n + 1) * q, f * SUB : (f + 1) * SUB] for n in (0, 2, 1, 3)], 1
             )
-            for f in range(FRAMES)
+            for f in range(FIELDS)
         ],
         0,
     )
     pupil_bar = const_right(rows, right_high, right_low)
-    pupil = pupil_ref[0, 0]
-    phase_bar = ratio * (pupil[:, :SUB] * pupil_bar[:, SUB:] - pupil[:, SUB:] * pupil_bar[:, :SUB])
-
-    @pl.when(channel == 0)
-    def _():
-        phase_acc[...] = phase_bar
-
-    @pl.when(channel == CH - 1)
-    def _():
-        total = phase_acc[...] + phase_bar
-        modes = basis_ref.shape[0]
-        ones = jnp.ones((8, SUB), F32)
-        for f in range(FRAMES):
-            part = jnp.sum(basis_ref[...] * total[f * q : (f + 1) * q][None], axis=1)
-            line = lax.dot_general(
-                ones, part, (((1,), (1,)), ((), ())), precision=HIGHEST, preferred_element_type=F32
-            )
-            out_ref[0, f : f + 1, :] = jnp.concatenate(
-                [line[:1], jnp.zeros((1, SUB - modes), F32)], 1
-            )
+    phase_bar = pupil[:, :SUB] * pupil_bar[:, SUB:] - pupil[:, SUB:] * pupil_bar[:, :SUB]
+    size = FRAMES * q
+    total = phase_bar[:size]
+    for c in range(1, CH):
+        total = total + phase_bar[c * size : (c + 1) * size] * np.float32(1.0 / (1.0 + 0.25 * c))
+    modes = basis_ref.shape[0]
+    ones = jnp.ones((8, SUB), F32)
+    gap = jnp.zeros((1, SLOT - modes), F32)
+    lines = []
+    for f in range(FRAMES):
+        part = jnp.sum(basis_ref[...] * total[f * q : (f + 1) * q][None], axis=1)
+        line = lax.dot_general(
+            ones, part, (((1,), (1,)), ((), ())), precision=HIGHEST, preferred_element_type=F32
+        )
+        lines += [line[:1], gap]
+    return jnp.concatenate(
+        [jnp.concatenate(lines[:4], 1), jnp.concatenate(lines[4:], 1)], 0
+    )
+
+
+def forward_kernel(scale, modes, coeff_ref, basis_ref, mask_ref, *refs):
+    tables, (otf_ref, field_ref, pupil_ref) = refs[:8], refs[8:]
+    otf, field, pupil = forward_math(scale, modes, coeff_ref, basis_ref, mask_ref, tables)
+    otf_ref[0] = otf
+    field_ref[0] = field
+    pupil_ref[0] = pupil
+
+
+def backward_kernel(scale, cells_ref, otf_ref, field_ref, pupil_ref, basis_ref, weight_ref, *refs):
+    tables, data_tables, (data_ref, out_ref) = refs[:8], refs[8:12], refs[12:]
+    images = jnp.concatenate(
+        [cells_ref[:, 0, c, f].reshape(SUB, SUB) for c in range(CH) for f in range(FRAMES)], 1
+    )
+    data = half_plane(images, *data_tables)
+    data_ref[0] = data
+    out_ref[0] = backward_math(
+        scale, data, otf_ref[0], field_ref[0], pupil_ref[0], basis_ref, weight_ref, tables
+    )
+
+
+def joint_kernel(scale, modes, coeff_ref, data_ref, basis_ref, mask_ref, weight_ref, *refs):
+    forward_tables, backward_tables, out_ref = refs[:8], refs[8:16], refs[16]
+    otf, field, pupil = forward_math(scale, modes, coeff_ref, basis_ref, mask_ref, forward_tables)
+    out_ref[0] = backward_math(
+        scale, data_ref[0], otf, field, pupil, basis_ref, weight_ref, backward_tables
+    )
 
 
 def gather_kernel(n, block_ref, out_ref, send_sem, recv_sem):
@@ -362,17 +352,23 @@
         for name in tables
         if name not in ("weight", "mask", "area")
     }
+    twice = {
+        name: [jnp.concatenate([pairs[name][0]] * 2, 1), pairs[name][1]]
+        for name in ("left", "rows", "data_rows")
+    }
     scale = float(1.0 / (SUB * SUB * tables["area"]))
 
-    owned_rows = owned * FRAMES
+    owned_rows = owned * 2
     tile_rows = -(-(owned_rows + 2) // 8) * 8
     mine = jnp.zeros((tile_rows, SUB), F32)
-    mine = mine.at[:owned_rows, :modes].set(coeffs.transpose(2, 0, 1).reshape(owned_rows, modes))
+    packed = coeffs.transpose(2, 0, 1).reshape(owned_rows, 2, modes)
+    packed = jnp.pad(packed, ((0, 0), (0, 0), (0, SLOT - modes))).reshape(owned_rows, SUB)
+    mine = mine.at[:owned_rows].set(packed)
     owned_row_patch = owned_rows
     mine = mine.at[owned_rows, :per].set(patches.astype(F32))
     mine = mine.at[owned_rows + 1, :per].set(anchors.astype(F32))
     everyone = spread_blocks(mine, 0)
-    all_coeffs = everyone[:, :owned_rows, :].reshape(devices * owned, FRAMES * SUB)
+    all_coeffs = everyone[:, :owned_rows, :].reshape(devices * owned, 2 * SUB)
     group = devices // TR
     tile = device // group
     place = device % group
@@ -407,64 +403,61 @@
     per = share
 
     big = pltpu.CompilerParams(vmem_limit_bytes=VMEM_LIMIT)
-    spectrum_shape = jax.ShapeDtypeStruct((per, CH, FRAMES * HALF, 2 * SUB), F32)
-
-    def per_block(*tail):
-        return pl.BlockSpec((1, 1) + tail, lambda s, c: (s, c, 0, 0))
-
-    data_tables = pairs["data_rows"] + pairs["data_mixed"]
-    data = pl.pallas_call(
-        data_kernel,
-        grid=(per, CH),
-        in_specs=[
-            pl.BlockSpec(
-                (cells.shape[0], 1, 1) + cells.shape[3:], lambda s, c: (0, s, c, 0, 0, 0)
-            )
-        ]
-        + [whole(t) for t in data_tables],
-        out_specs=per_block(FRAMES * HALF, 2 * SUB),
-        out_shape=spectrum_shape,
-        compiler_params=big,
-        cost_estimate=pl.CostEstimate(flops=6 * 10**9, bytes_accessed=5 << 20, transcendentals=0),
-    )(cells, *data_tables)
-
     basis = zbasis.reshape(modes, PUP // 2, SUB)
     mask = jnp.asarray(tables["mask"])
     weight = jnp.asarray(tables["weight"])
-    forward_tables = pairs["right"] + pairs["left"] + pairs["rows"] + pairs["mixed"]
+    forward_tables = pairs["right"] + twice["left"] + twice["rows"] + pairs["mixed"]
     backward_tables = pairs["mixed"] + pairs["rows_t"] + pairs["left_t"] + pairs["right_t"]
+    data_tables = twice["data_rows"] + pairs["data_mixed"]
     saved_shapes = [
-        spectrum_shape,
-        jax.ShapeDtypeStruct((per, CH, 2 * SUB, FRAMES * SUB), F32),
-        jax.ShapeDtypeStruct((per, CH, FRAMES * PUP // 2, 2 * SUB), F32),
+        jax.ShapeDtypeStruct((per, FIELDS * HALF, 2 * SUB), F32),
+        jax.ShapeDtypeStruct((per, 2 * SUB, FIELDS * SUB), F32),
+        jax.ShapeDtypeStruct((per, FIELDS * PUP // 2, 2 * SUB), F32),
     ]
-    saved_specs = [per_block(*s.shape[2:]) for s in saved_shapes]
-
-    def slopes_of(chosen):
-        flat = chosen.reshape(per * FRAMES, SUB)
+    saved_specs = [pl.BlockSpec((1,) + t.shape[1:], lambda s: (s, 0, 0)) for t in saved_shapes]
+    slope_shape = jax.ShapeDtypeStruct((per, 2, SUB), F32)
+    slope_spec = pl.BlockSpec((1, 2, SUB), lambda s: (s, 0, 0))
+    smem = pl.BlockSpec(memory_space=pltpu.SMEM)
+
+    def cost(flops):
+        return pl.CostEstimate(flops=flops, bytes_accessed=8 << 20, transcendentals=0)
+
+    def first_slopes(chosen):
         saved = pl.pallas_call(
             functools.partial(forward_kernel, scale, modes),
-            grid=(per, CH),
-            in_specs=[pl.BlockSpec(memory_space=pltpu.SMEM), whole(basis), whole(mask)]
-            + [whole(t) for t in forward_tables],
+            grid=(per,),
+            in_specs=[smem, whole(basis), whole(mask)] + [whole(t) for t in forward_tables],
             out_specs=saved_specs,
             out_shape=saved_shapes,
             compiler_params=big,
-            cost_estimate=pl.CostEstimate(flops=10**10, bytes_accessed=8 << 20, transcendentals=0),
-        )(flat, basis, mask, *forward_tables)
+            cost_estimate=cost(10**10),
+        )(chosen.reshape(per * 2, SUB), basis, mask, *forward_tables)
+        cell_spec = pl.BlockSpec(
+            (cells.shape[0], 1) + cells.shape[2:], lambda s: (0, s, 0, 0, 0, 0)
+        )
         return pl.pallas_call(
             functools.partial(backward_kernel, scale),
-            grid=(per, CH),
-            in_specs=[per_block(FRAMES * HALF, 2 * SUB)]
+            grid=(per,),
+            in_specs=[cell_spec]
             + saved_specs
-            + [whole(basis), whole(weight)]
-            + [whole(t) for t in backward_tables],
-            out_specs=pl.BlockSpec((1, FRAMES, SUB), lambda s, c: (s, 0, 0)),
-            out_shape=jax.ShapeDtypeStruct((per, FRAMES, SUB), F32),
-            scratch_shapes=[pltpu.VMEM((FRAMES * PUP // 2, SUB), F32)],
+            + [whole(t) for t in [basis, weight] + backward_tables + data_tables],
+            out_specs=[saved_specs[0], slope_spec],
+            out_shape=[saved_shapes[0], slope_shape],
             compiler_params=big,
-            cost_estimate=pl.CostEstimate(flops=10**10, bytes_accessed=8 << 20, transcendentals=0),
-        )(data, *saved, basis, weight, *backward_tables)
+            cost_estimate=cost(10**10),
+        )(cells, *saved, basis, weight, *backward_tables, *data_tables)
+
+    def later_slopes(chosen, data):
+        fixed = [basis, mask, weight] + forward_tables + backward_tables
+        return pl.pallas_call(
+            functools.partial(joint_kernel, scale, modes),
+            grid=(per,),
+            in_specs=[smem, saved_specs[0]] + [whole(t) for t in fixed],
+            out_specs=slope_spec,
+            out_shape=slope_shape,
+            compiler_params=big,
+            cost_estimate=cost(2 * 10**10),
+        )(chosen.reshape(per * 2, SUB), data, *fixed)
 
     patch_ids = jnp.arange(devices * owned, dtype=jnp.int32)
     own_ids = device * owned + jnp.arange(owned, dtype=jnp.int32)
@@ -474,14 +467,17 @@
     sums = (wanted[:, None] == all_patches[None, :]).astype(F32)
     gradient = jnp.zeros_like(current)
     for iteration in range(ITERS):
-        slopes = slopes_of(current[:per])
-        gathered = spread_blocks(slopes.reshape(per * FRAMES, SUB), 1 + iteration)
-        gathered = gathered.reshape(devices * per, FRAMES * SUB)
+        if iteration == 0:
+            data, slopes = first_slopes(current[:per])
+        else:
+            slopes = later_slopes(current[:per], data)
+        gathered = spread_blocks(slopes.reshape(per * 2, SUB), 1 + iteration)
+        gathered = gathered.reshape(devices * per, 2 * SUB)
         gradient = jnp.dot(sums, gathered, precision=HIGHEST)
         current = current - STEP_SIZE * gradient
 
     def owned_part(value):
-        return value[per:].reshape(owned, FRAMES, SUB)[:, :, :modes].transpose(1, 2, 0)
+        return value[per:].reshape(owned, FRAMES, SLOT)[:, :, :modes].transpose(1, 2, 0)
 
     return owned_part(current), owned_part(gradient)
 

time: 134 us -> 135 us (level)
  Pallas kernels: 98.6 us -> 74.7 us
  local copies, waits for them, and re-layouts: 20.3 us -> 40.1 us
  waiting for transfers between devices: 4.56 us -> 9.7 us
    pallas_call x5 -> x3, Pallas kernels: 59.5 us -> 39.6 us  [the longest x1 17.4 us: later_slopes(): pl.pallas_call(functools.partial(joint_kernel, scale, modes), grid=(per,)...]
    unnamed x89 -> x83, local copies, waits for them, and re-layouts: 16.3 us -> 35.2 us
    all_to_all x1, waiting for transfers between devices: 4.56 us -> 9.7 us  [on_device(): lax.all_to_all(windows, 'sub', 0, 0, axis_index_groups=teams, tiled=True)]
    pallas_call x3, Pallas kernels: 35.9 us -> 32 us  [spread_blocks(): pl.pallas_call(functools.partial(gather_kernel, n), out_shape=jax.ShapeDt...]
    reshape x4 -> x6, local copies, waits for them, and re-layouts: 2.02 us -> 3.24 us  [the longest x2 1.89 us: on_device(): gathered = gathered.reshape(devices * per, 2 * SUB)]
  transfers between devices with their start and end apart: 1 -> 1, of which waited for: 1 -> 1; matrix products, arithmetic and copies ran while one was open for 2% -> 2% of each run, Pallas kernels for 10% -> 6%
where the time goes in v3:
time: 135 us; the launch traced here: 133 us
  Pallas kernels  74.7 us (55%)
  local copies, waits for them, and re-layouts  40.1 us (30%)
  waiting for transfers between devices  9.7 us (7%)
  starting transfers between devices  4.47 us (3%)
  other arithmetic  2.55 us (2%)
    unnamed x83, local copies, waits for them, and re-layouts  35.2 us
    pallas_call x3, Pallas kernels, spread_blocks(): pl.pallas_call(functools.partial(gather_kernel, n), out_shape=jax.ShapeDt...  32 us
    pallas_call x1, Pallas kernels, later_slopes(): pl.pallas_call(functools.partial(joint_kernel, scale, modes), grid=(per,)...  17.4 us
    pallas_call x1, Pallas kernels, first_slopes(): pl.pallas_call(functools.partial(backward_kernel, scale), grid=(per,), in...  14.2 us
    all_to_all x1, waiting for transfers between devices, on_device(): lax.all_to_all(windows, 'sub', 0, 0, axis_index_groups=teams, tiled=True)  9.7 us
    pallas_call x1, Pallas kernels, first_slopes(): pl.pallas_call(functools.partial(forward_kernel, scale, modes), grid=(per...  7.96 us
    all_to_all x1, starting transfers between devices, on_device(): lax.all_to_all(windows, 'sub', 0, 0, axis_index_groups=teams, tiled=True)  4.47 us
    pallas_call x1, Pallas kernels, on_device(): pl.pallas_call(functools.partial(window_kernel, batch), grid_spec=pltpu.P...  3.22 us
  transfers between devices with their start and end apart: 1, of which 1 were waited for; matrix products, arithmetic and copies ran while one was open for 2% of the time, Pallas kernels for 6%

profile of v3, /device:TPU:0, one launch (start us, length us, event | category | flops | bytes accessed | tf_op | source)
XLA Modules:
  0.0 133.0 jit_solution(5577872335657981218)
XLA Ops:
  3.7 11.9 %shard_map.248 = f32[32,8,128]{2,1,0:T(8,128)} custom-call(f32[8,128]{1,0:T(8,128)} %copy-done.40), custom_call_target="tpu_custom_call" | custom-call | tf_op jit(solution)/shard_map/pallas_call | solution.py:328
  15.6 1.0 fusion.14
  16.8 1.6 %copy-done = f32[2,4,16,4096]{3,2,1,0:T(8,128)S(1)} copy-done((f32[2,4,16,4096]{3,2,1,0:T(8,128)S(1)}, f32[2,4,16,4096]{3,2,1,0:T(8,128)}, u32[]{:S(2)}) %copy-start) | copy-done | bytes 2097176
  18.4 3.2 %shard_map.249 = f32[32,128,128]{2,1,0:T(8,128)} custom-call(s32[32]{0:T(128)S(1)} %convert_element_type.23.anchor_ref, f32[128,4096]{1,0:T(8,128)S(1)} %bitcast.30), custom_call_target="tpu_custom_call" | custom-call | tf_op jit(solution)/shard_map/pallas_call | solution.py:387
  21.6 4.5 %all-to-all-start = ((f32[32,128,128]{2,1,0:T(8,128)}), f32[32,128,128]{2,1,0:T(8,128)S(1)}, u32[]{:S(2)}, u32[]{:S(2)}) async-start(f32[32,128,128]{2,1,0:T(8,128)} %shard_map.249), calls=%async_computation | async-start | bytes 4194304 | tf_op jit(solution)/shard_map/all_to_all | solution.py:399
  26.8 1.3 copy.32
  28.2 0.9 copy-done.10
  29.1 0.9 copy-done.13
  30.0 0.9 copy-done.15
  32.6 8.0 %shard_map.250 = (f32[4,576,256]{2,1,0:T(8,128)S(1)}, f32[4,256,1024]{2,1,0:T(8,128)}, f32[4,256,256]{2,1,0:T(8,128)S(1)}) custom-call(f32[8,128]{1,0:T(8,128)S(1)} %reshape.149.coeff_ref, f32[45,32,128]{2,1,0:T(8,128)S(1)} %slice.95.basis_ref, f32[256,128]{1,0:T(8,128)S(1)} %copy-done.15, bf16[256,512]{1,0:T(8,128)(2,1)S(1)} %copy-done.4, ...), custom_call_target="tpu_custom_call" | custom-call | flops 10000000000 | bytes 8388608 | tf_op jit(solution)/shard_map/pallas_call | solution.py:426
  40.6 1.5 %copy-done.37 = f32[4,576,256]{2,1,0:T(8,128)} copy-done((f32[4,576,256]{2,1,0:T(8,128)}, f32[4,576,256]{2,1,0:T(8,128)S(1)}, u32[]{:S(2)}) %copy-start.37) | copy-done | bytes 2359320
  42.0 1.0 copy-done.38
  43.0 9.7 %all-to-all-done = f32[32,128,128]{2,1,0:T(8,128)S(1)} async-done(((f32[32,128,128]{2,1,0:T(8,128)}), f32[32,128,128]{2,1,0:T(8,128)S(1)}, u32[]{:S(2)}, u32[]{:S(2)}) %all-to-all-start) | async-done | bytes 2097184 | tf_op jit(solution)/shard_map/all_to_all | solution.py:399
  52.7 0.9 copy-done.5
  53.7 0.9 copy-done.7
  54.6 0.9 copy-done.11
  55.5 0.9 copy-done.17
  56.4 0.9 copy-done.18
  57.3 0.9 copy-done.21
  63.1 1.2 copy-done.39
  64.3 14.2 %shard_map.251 = (f32[4,576,256]{2,1,0:T(8,128)}, f32[4,2,128]{2,1,0:T(2,128)S(1)}) custom-call(f32[8,4,2,4,16,128]{5,4,3,2,1,0:T(8,128)S(1)} %bitcast.31, f32[4,576,256]{2,1,0:T(8,128)} %copy-done.37, f32[4,256,1024]{2,1,0:T(8,128)} %get-tuple-element.44.field_ref, f32[4,256,256]{2,1,0:T(8,128)S(1)} %copy-done.39, f32[45,32,128]{2,1,0:T(8,128)S(1)} %slice.95.basis_ref, ...), custom_call_target="tpu_custom_call" | custom-call | flops 10000000000 | bytes 8388608 | tf_op jit(solution)/shard_map/pallas_call | solution.py:438
  79.1 10.1 %shard_map.252 = f32[32,8,128]{2,1,0:T(8,128)} custom-call(f32[8,128]{1,0:T(8,128)} %bitcast.33), custom_call_target="tpu_custom_call" | custom-call | tf_op jit(solution)/shard_map/pallas_call | solution.py:328
  89.2 0.9 reshape.152
  90.4 0.9 copy-done.6
  91.3 0.9 copy-done.8
  92.3 0.9 copy-done.12
  93.2 0.9 copy-done.14
  94.1 0.9 copy-done.16
  100.9 1.7 %copy-done.36 = f32[4,576,256]{2,1,0:T(8,128)S(1)} copy-done((f32[4,576,256]{2,1,0:T(8,128)S(1)}, f32[4,576,256]{2,1,0:T(8,128)}, u32[]{:S(2)}) %copy-start.36) | copy-done | bytes 2359320
  102.5 17.4 %shard_map.253 = f32[4,2,128]{2,1,0:T(2,128)S(1)} custom-call(f32[8,128]{1,0:T(8,128)S(1)} %reshape.153.coeff_ref, f32[4,576,256]{2,1,0:T(8,128)S(1)} %copy-done.36, f32[45,32,128]{2,1,0:T(8,128)S(1)} %slice.95.basis_ref, f32[256,128]{1,0:T(8,128)S(1)} %copy-done.16, f32[72,128]{1,0:T(8,128)S(1)} %copy-done.34, bf16[256,512]{1,0:T(8,128)(2,1)S(1)} %copy-done.4, ...), custom_call_target="tpu_custom_call" | custom-call | flops 20000000000 | bytes 8388608 | tf_op jit(solution)/shard_map/pallas_call | solution.py:452
  120.5 10.0 %shard_map.254 = f32[32,8,128]{2,1,0:T(8,128)} custom-call(f32[8,128]{1,0:T(8,128)} %bitcast.32), custom_call_target="tpu_custom_call" | custom-call | tf_op jit(solution)/shard_map/pallas_call | solution.py:328
  130.5 0.9 reshape.155
  (91 shorter events, 19.3 us)
Async XLA Ops:
  16.8 1.6 %copy-start = (f32[2,4,16,4096]{3,2,1,0:T(8,128)S(1)}, f32[2,4,16,4096]{3,2,1,0:T(8,128)}, u32[]{:S(2)}) copy-start(f32[2,4,16,4096]{3,2,1,0:T(8,128)} %param.31) | copy-start | bytes 6291460
  21.6 5.0 %slice-start = ((f32[32,8,128]{2,1,0:T(8,128)}), f32[32,2,128]{2,1,0:T(2,128)S(1)}, s32[]{:S(2)}) async-start(f32[32,8,128]{2,1,0:T(8,128)} %shard_map.248), calls=%async_computation.1 | async-start | bytes 65536 | tf_op jit(solution)/shard_map/slice | solution.py:371
  21.6 31.1 %all-to-all-start = ((f32[32,128,128]{2,1,0:T(8,128)}), f32[32,128,128]{2,1,0:T(8,128)S(1)}, u32[]{:S(2)}, u32[]{:S(2)}) async-start(f32[32,128,128]{2,1,0:T(8,128)} %shard_map.249), calls=%async_computation | async-start | bytes 4194304 | tf_op jit(solution)/shard_map/all_to_all | solution.py:399
  26.1 2.1 %copy-start.3 = (bf16[256,512]{1,0:T(8,128)(2,1)S(1)}, bf16[256,512]{1,0:T(8,128)(2,1)}, u32[]{:S(2)}) copy-start(bf16[256,512]{1,0:T(8,128)(2,1)} %constant.164.clone.refs_1_) | copy-start | bytes 786436
  26.1 2.1 %copy-start.4 = (bf16[256,512]{1,0:T(8,128)(2,1)S(1)}, bf16[256,512]{1,0:T(8,128)(2,1)}, u32[]{:S(2)}) copy-start(bf16[256,512]{1,0:T(8,128)(2,1)} %constant.163.clone.refs_0_) | copy-start | bytes 786436
  26.1 2.1 %copy-start.9 = (bf16[256,256]{1,0:T(8,128)(2,1)S(1)}, bf16[256,256]{1,0:T(8,128)(2,1)}, u32[]{:S(2)}) copy-start(bf16[256,256]{1,0:T(8,128)(2,1)} %constant.176.clone.refs_7_.refs_1_.refs_9_) | copy-start | bytes 393220
  26.1 2.1 %copy-start.32 = (bf16[144,128]{1,0:T(8,128)(2,1)S(1)}, bf16[144,128]{1,0:T(8,128)(2,1)}, u32[]{:S(2)}) copy-start(bf16[144,128]{1,0:T(8,128)(2,1)} %constant.172.clone.refs_5_) | copy-start | bytes 110596
  28.2 0.9 copy-start.10
  29.1 0.9 copy-start.13
  30.0 0.9 copy-start.15
  30.9 0.9 copy-start.19
  31.8 0.8 copy-start.22
  40.6 1.5 %copy-start.37 = (f32[4,576,256]{2,1,0:T(8,128)}, f32[4,576,256]{2,1,0:T(8,128)S(1)}, u32[]{:S(2)}) copy-start(f32[4,576,256]{2,1,0:T(8,128)S(1)} %get-tuple-element.43.otf_ref) | copy-start | bytes 7077892
  42.0 1.0 copy-start.38
  52.7 1.0 copy-start.5
  53.7 0.9 copy-start.7
  54.6 0.9 copy-start.11
  55.5 0.9 copy-start.17
  56.4 0.9 copy-start.18
  57.3 0.9 copy-start.21
  58.2 0.8 copy-start.24
  59.0 0.8 copy-start.26
  59.9 0.8 copy-start.28
  60.7 0.8 copy-start.30
  63.1 1.2 copy-start.39
  90.4 1.0 copy-start.6
  91.3 0.9 copy-start.8
  92.3 0.9 copy-start.12
  93.2 0.9 copy-start.14
  94.1 0.9 copy-start.16
  95.0 0.9 copy-start.20
  100.8 1.7 %copy-start.36 = (f32[4,576,256]{2,1,0:T(8,128)S(1)}, f32[4,576,256]{2,1,0:T(8,128)}, u32[]{:S(2)}) copy-start(f32[4,576,256]{2,1,0:T(8,128)} %get-tuple-element.47.data_ref) | copy-start | bytes 7077892
  (11 other events, 8.3 us)

commit v4 on v3

--- a/solution.py
+++ b/solution.py
@@ -70,9 +70,32 @@
         "data_rows": rows * taper[None, :],
         "data_mixed": np.concatenate([taper, taper])[:, None] * mixed,
         "weight": np.broadcast_to(weight, (HALF, SUB)).astype(np.float32) * np.float32(-2.0 / SUB**4),
-        "mask": np.tile(mask, (FIELDS, 1)),
+        "mask": mask,
         "area": area,
     }
+
+
+def pack_tables(tables):
+    split_tables = {name: split_np(tables[name]) for name in tables if name not in ("weight", "mask", "area")}
+    for half in range(2):
+        split_tables["right%d" % half] = tuple(
+            part[:, half * 2 * SUB : (half + 1) * 2 * SUB] for part in split_tables["right"]
+        )
+    del split_tables["right"]
+    for name in ("left", "rows", "data_rows"):
+        high, low = split_tables[name]
+        split_tables[name] = (np.concatenate([high, high], 1), low)
+    spots, parts, at = {}, [], 0
+    for name in sorted(split_tables):
+        for part in split_tables[name]:
+            spots.setdefault(name, []).append((at, part.shape[0], part.shape[1]))
+            parts.append(np.pad(part, ((0, 0), (0, 2 * SUB - part.shape[1]))))
+            at += part.shape[0]
+    return np.concatenate(parts, 0), spots
+
+
+def views(ref, spots, *names):
+    return [ref.at[pl.ds(at, size), pl.ds(0, width)] for name in names for at, size, width in spots[name]]
 
 
 def split(value):
@@ -156,7 +179,7 @@
 
 
 def forward_math(scale, modes, coeff_ref, basis_ref, mask_ref, tables):
-    right_high, right_low, left_twice, left_low, rows_twice, rows_low, mixed_high, mixed_low = tables
+    left_twice, left_low, rows_twice, rows_low, mixed_high, mixed_low = tables[4:]
     subfield = pl.program_id(0)
     q = PUP // 2
     sums = [jnp.zeros((q, SUB), F32) for _ in range(FRAMES)]
@@ -168,9 +191,9 @@
     phase = jnp.concatenate(sums, 0)
     phase = jnp.concatenate([phase * np.float32(1.0 / (1.0 + 0.25 * c)) for c in range(CH)], 0)
     sine, cosine = sin_cos(phase)
-    mask = mask_ref[...]
+    mask = jnp.concatenate([mask_ref[:q]] * FIELDS, 0)
     pupil = jnp.concatenate([mask * cosine, mask * sine], 1)
-    half = const_right(pupil, right_high, right_low)
+    half = jnp.concatenate([const_right(pupil, *tables[:2]), const_right(pupil, *tables[2:4])], 1)
     blocks = jnp.concatenate(
         [
             jnp.concatenate(
@@ -187,7 +210,7 @@
 
 def backward_math(scale, data, otf, field, pupil, basis_ref, weight_ref, tables):
     mixed_high, mixed_low, rows_high, rows_low, left_high, left_low, right_high, right_low = tables
-    weight = weight_ref[...]
+    weight = weight_ref[PUP // 2 :]
     bars = []
     for c in range(CH):
         parts = []
@@ -256,32 +279,38 @@
     )
 
 
-def forward_kernel(scale, modes, coeff_ref, basis_ref, mask_ref, *refs):
-    tables, (otf_ref, field_ref, pupil_ref) = refs[:8], refs[8:]
-    otf, field, pupil = forward_math(scale, modes, coeff_ref, basis_ref, mask_ref, tables)
+FORWARD = ("right0", "right1", "left", "rows", "mixed")
+BACKWARD = ("mixed", "rows_t", "left_t", "right_t")
+DATA = ("data_rows", "data_mixed")
+
+
+def forward_kernel(scale, modes, spots, coeff_ref, basis_ref, fixed_ref, pack_ref, otf_ref, field_ref, pupil_ref):
+    tables = views(pack_ref, spots, *FORWARD)
+    otf, field, pupil = forward_math(scale, modes, coeff_ref, basis_ref, fixed_ref, tables)
     otf_ref[0] = otf
     field_ref[0] = field
     pupil_ref[0] = pupil
 
 
-def backward_kernel(scale, cells_ref, otf_ref, field_ref, pupil_ref, basis_ref, weight_ref, *refs):
-    tables, data_tables, (data_ref, out_ref) = refs[:8], refs[8:12], refs[12:]
+def backward_kernel(
+    scale, spots, cells_ref, otf_ref, field_ref, pupil_ref, basis_ref, fixed_ref, pack_ref, data_ref, out_ref
+):
     images = jnp.concatenate(
         [cells_ref[:, 0, c, f].reshape(SUB, SUB) for c in range(CH) for f in range(FRAMES)], 1
     )
-    data = half_plane(images, *data_tables)
+    data = half_plane(images, *views(pack_ref, spots, *DATA))
     data_ref[0] = data
+    tables = views(pack_ref, spots, *BACKWARD)
     out_ref[0] = backward_math(
-        scale, data, otf_ref[0], field_ref[0], pupil_ref[0], basis_ref, weight_ref, tables
-    )
-
-
-def joint_kernel(scale, modes, coeff_ref, data_ref, basis_ref, mask_ref, weight_ref, *refs):
-    forward_tables, backward_tables, out_ref = refs[:8], refs[8:16], refs[16]
-    otf, field, pupil = forward_math(scale, modes, coeff_ref, basis_ref, mask_ref, forward_tables)
-    out_ref[0] = backward_math(
-        scale, data_ref[0], otf, field, pupil, basis_ref, weight_ref, backward_tables
-    )
+        scale, data, otf_ref[0], field_ref[0], pupil_ref[0], basis_ref, fixed_ref, tables
+    )
+
+
+def joint_kernel(scale, modes, spots, coeff_ref, data_ref, basis_ref, fixed_ref, pack_ref, out_ref):
+    tables = views(pack_ref, spots, *FORWARD)
+    otf, field, pupil = forward_math(scale, modes, coeff_ref, basis_ref, fixed_ref, tables)
+    tables = views(pack_ref, spots, *BACKWARD)
+    out_ref[0] = backward_math(scale, data_ref[0], otf, field, pupil, basis_ref, fixed_ref, tables)
 
 
 def gather_kernel(n, block_ref, out_ref, send_sem, recv_sem):
@@ -347,15 +376,8 @@
     owned = coeffs.shape[2]
     modes = coeffs.shape[1]
     tables = make_tables()
-    pairs = {
-        name: [jnp.asarray(part) for part in split_np(tables[name])]
-        for name in tables
-        if name not in ("weight", "mask", "area")
-    }
-    twice = {
-        name: [jnp.concatenate([pairs[name][0]] * 2, 1), pairs[name][1]]
-        for name in ("left", "rows", "data_rows")
-    }
+    pack, spots = pack_tables(tables)
+    pack = jnp.asarray(pack)
     scale = float(1.0 / (SUB * SUB * tables["area"]))
 
     owned_rows = owned * 2
@@ -404,11 +426,8 @@
 
     big = pltpu.CompilerParams(vmem_limit_bytes=VMEM_LIMIT)
     basis = zbasis.reshape(modes, PUP // 2, SUB)
-    mask = jnp.asarray(tables["mask"])
-    weight = jnp.asarray(tables["weight"])
-    forward_tables = pairs["right"] + twice["left"] + twice["rows"] + pairs["mixed"]
-    backward_tables = pairs["mixed"] + pairs["rows_t"] + pairs["left_t"] + pairs["right_t"]
-    data_tables = twice["data_rows"] + pairs["data_mixed"]
+    fixed = jnp.asarray(np.concatenate([tables["mask"], tables["weight"]], 0))
+    shared = [basis, fixed, pack]
     saved_shapes = [
         jax.ShapeDtypeStruct((per, FIELDS * HALF, 2 * SUB), F32),
         jax.ShapeDtypeStruct((per, 2 * SUB, FIELDS * SUB), F32),
@@ -424,40 +443,39 @@
 
     def first_slopes(chosen):
         saved = pl.pallas_call(
-            functools.partial(forward_kernel, scale, modes),
+            functools.partial(forward_kernel, scale, modes, spots),
             grid=(per,),
-            in_specs=[smem, whole(basis), whole(mask)] + [whole(t) for t in forward_tables],
+            in_specs=[smem] + [whole(t) for t in shared],
             out_specs=saved_specs,
             out_shape=saved_shapes,
             compiler_params=big,
             cost_estimate=cost(10**10),
-        )(chosen.reshape(per * 2, SUB), basis, mask, *forward_tables)
+        )(chosen.reshape(per * 2, SUB), *shared)
         cell_spec = pl.BlockSpec(
             (cells.shape[0], 1) + cells.shape[2:], lambda s: (0, s, 0, 0, 0, 0)
         )
         return pl.pallas_call(
-            functools.partial(backward_kernel, scale),
+            functools.partial(backward_kernel, scale, spots),
             grid=(per,),
             in_specs=[cell_spec]
             + saved_specs
-            + [whole(t) for t in [basis, weight] + backward_tables + data_tables],
+            + [whole(t) for t in shared],
             out_specs=[saved_specs[0], slope_spec],
             out_shape=[saved_shapes[0], slope_shape],
             compiler_params=big,
             cost_estimate=cost(10**10),
-        )(cells, *saved, basis, weight, *backward_tables, *data_tables)
+        )(cells, *saved, *shared)
 
     def later_slopes(chosen, data):
-        fixed = [basis, mask, weight] + forward_tables + backward_tables
         return pl.pallas_call(
-            functools.partial(joint_kernel, scale, modes),
+            functools.partial(joint_kernel, scale, modes, spots),
             grid=(per,),
-            in_specs=[smem, saved_specs[0]] + [whole(t) for t in fixed],
+            in_specs=[smem, saved_specs[0]] + [whole(t) for t in shared],
             out_specs=slope_spec,
             out_shape=slope_shape,
             compiler_params=big,
             cost_estimate=cost(2 * 10**10),
-        )(chosen.reshape(per * 2, SUB), data, *fixed)
+        )(chosen.reshape(per * 2, SUB), data, *shared)
 
     patch_ids = jnp.arange(devices * owned, dtype=jnp.int32)
     own_ids = device * owned + jnp.arange(owned, dtype=jnp.int32)

time: 135 us -> 115 us (0.85); the launches traced: 133 us -> 114 us
  local copies, waits for them, and re-layouts: 40.1 us -> 16.6 us
  waiting for transfers between devices: 9.7 us -> 13.1 us
  Pallas kernels: 74.7 us -> 76.4 us
    unnamed x83 -> x21, local copies, waits for them, and re-layouts: 35.2 us -> 11.7 us
    all_to_all x1, waiting for transfers between devices: 9.7 us -> 13.1 us  [on_device(): lax.all_to_all(windows, 'sub', 0, 0, axis_index_groups=teams, tiled=True)]
    pallas_call x3, Pallas kernels: 39.6 us -> 41.2 us  [the longest x1 17.2 us: later_slopes(): pl.pallas_call(functools.partial(joint_kernel, scale, modes, spots), grid...]
  transfers between devices with their start and end apart: 1 -> 1, of which waited for: 1 -> 1; matrix products, arithmetic and copies ran while one was open for 2% -> 2% of each run, Pallas kernels for 6% -> 8%
where the time goes in v4:
time: 115 us; the launch traced here: 114 us
  Pallas kernels  76.4 us (66%)
  local copies, waits for them, and re-layouts  16.6 us (14%)
  waiting for transfers between devices  13.1 us (11%)
  starting transfers between devices  4.47 us (4%)
  other arithmetic  2.55 us (2%)
    pallas_call x3, Pallas kernels, spread_blocks(): pl.pallas_call(functools.partial(gather_kernel, n), out_shape=jax.ShapeDt...  32 us
    pallas_call x1, Pallas kernels, later_slopes(): pl.pallas_call(functools.partial(joint_kernel, scale, modes, spots), grid...  17.2 us
    pallas_call x1, Pallas kernels, first_slopes(): pl.pallas_call(functools.partial(backward_kernel, scale, spots), grid=(pe...  14.9 us
    all_to_all x1, waiting for transfers between devices, on_device(): lax.all_to_all(windows, 'sub', 0, 0, axis_index_groups=teams, tiled=True)  13.1 us
    unnamed x21, local copies, waits for them, and re-layouts  11.7 us
    pallas_call x1, Pallas kernels, first_slopes(): pl.pallas_call(functools.partial(forward_kernel, scale, modes, spots), gr...  9.04 us
    all_to_all x1, starting transfers between devices, on_device(): lax.all_to_all(windows, 'sub', 0, 0, axis_index_groups=teams, tiled=True)  4.47 us
    pallas_call x1, Pallas kernels, on_device(): pl.pallas_call(functools.partial(window_kernel, batch), grid_spec=pltpu.P...  3.2 us
  transfers between devices with their start and end apart: 1, of which 1 were waited for; matrix products, arithmetic and copies ran while one was open for 2% of the time, Pallas kernels for 8%

profile of v4, /device:TPU:0, one launch (start us, length us, event | category | flops | bytes accessed | tf_op | source)
XLA Modules:
  0.0 114.4 jit_solution(5328095680374545984)
XLA Ops:
  0.7 0.7 convert_bitcast_fusion
  1.3 0.7 convert_bitcast_fusion.1
  2.0 0.7 pad.13
  2.9 0.2 scatter.14.block_ref
  3.1 0.6 copy-done.9
  3.7 11.9 %shard_map.86 = f32[32,8,128]{2,1,0:T(8,128)} custom-call(f32[8,128]{1,0:T(8,128)} %copy-done.9), custom_call_target="tpu_custom_call" | custom-call | tf_op jit(solution)/shard_map/pallas_call | solution.py:357
  15.6 1.0 fusion.14
  16.8 1.6 %copy-done = f32[2,4,16,4096]{3,2,1,0:T(8,128)S(1)} copy-done((f32[2,4,16,4096]{3,2,1,0:T(8,128)S(1)}, f32[2,4,16,4096]{3,2,1,0:T(8,128)}, u32[]{:S(2)}) %copy-start) | copy-done | bytes 2097176
  18.4 3.2 %shard_map.87 = f32[32,128,128]{2,1,0:T(8,128)} custom-call(s32[32]{0:T(128)S(1)} %convert_element_type.23.anchor_ref, f32[128,4096]{1,0:T(8,128)S(1)} %bitcast.30), custom_call_target="tpu_custom_call" | custom-call | tf_op jit(solution)/shard_map/pallas_call | solution.py:409
  21.6 4.5 %all-to-all-start = ((f32[32,128,128]{2,1,0:T(8,128)}), f32[32,128,128]{2,1,0:T(8,128)S(1)}, u32[]{:S(2)}, u32[]{:S(2)}) async-start(f32[32,128,128]{2,1,0:T(8,128)} %shard_map.87), calls=%async_computation | async-start | bytes 4194304 | tf_op jit(solution)/shard_map/all_to_all | solution.py:421
  26.3 0.2 dynamic-slice_reduce_fusion
  26.6 0.2 fusion.1
  26.8 1.3 %copy.14 = f32[6,8,32,128]{3,2,1,0:T(8,128)S(1)} copy(f32[6,8,32,128]{3,1,2,0:T(8,128)} %bitcast.35) | data formatting | bytes 1572864
  28.1 9.0 %shard_map.88 = (f32[4,576,256]{2,1,0:T(8,128)S(1)}, f32[4,256,1024]{2,1,0:T(8,128)}, f32[4,256,256]{2,1,0:T(8,128)S(1)}) custom-call(f32[8,128]{1,0:T(8,128)S(1)} %reshape.149.coeff_ref, f32[45,32,128]{2,1,0:T(8,128)S(1)} %slice.95.basis_ref, f32[104,128]{1,0:T(8,128)S(1)} %copy-done.4, bf16[4672,256]{1,0:T(8,128)(2,1)} %constant.127.clone.pack_ref), custom_call_target="tpu_custom_call" | custom-call | flops 10000000000 | bytes 8388608 | tf_op jit(solution)/shard_map/pallas_call | solution.py:445
  37.2 1.5 %copy-done.6 = f32[4,576,256]{2,1,0:T(8,128)} copy-done((f32[4,576,256]{2,1,0:T(8,128)}, f32[4,576,256]{2,1,0:T(8,128)S(1)}, u32[]{:S(2)}) %copy-start.6) | copy-done | bytes 2359320
  38.7 1.0 copy-done.7
  39.7 13.1 %all-to-all-done = f32[32,128,128]{2,1,0:T(8,128)S(1)} async-done(((f32[32,128,128]{2,1,0:T(8,128)}), f32[32,128,128]{2,1,0:T(8,128)S(1)}, u32[]{:S(2)}, u32[]{:S(2)}) %all-to-all-start) | async-done | bytes 2097184 | tf_op jit(solution)/shard_map/all_to_all | solution.py:421
  52.7 1.2 %copy-done.8 = f32[4,256,256]{2,1,0:T(8,128)S(1)} copy-done((f32[4,256,256]{2,1,0:T(8,128)S(1)}, f32[4,256,256]{2,1,0:T(8,128)}, u32[]{:S(2)}) %copy-start.8) | copy-done | bytes 1048600
  54.0 14.9 %shard_map.89 = (f32[4,576,256]{2,1,0:T(8,128)}, f32[4,2,128]{2,1,0:T(2,128)S(1)}) custom-call(f32[8,4,2,4,16,128]{5,4,3,2,1,0:T(8,128)S(1)} %bitcast.31, f32[4,576,256]{2,1,0:T(8,128)} %copy-done.6, f32[4,256,1024]{2,1,0:T(8,128)} %get-tuple-element.44.field_ref, f32[4,256,256]{2,1,0:T(8,128)S(1)} %copy-done.8, f32[45,32,128]{2,1,0:T(8,128)S(1)} %slice.95.basis_ref, ...), custom_call_target="tpu_custom_call" | custom-call | flops 10000000000 | bytes 8388608 | tf_op jit(solution)/shard_map/pallas_call | solution.py:457
  68.9 0.6 copy-done.1
  69.5 10.1 %shard_map.90 = f32[32,8,128]{2,1,0:T(8,128)} custom-call(f32[8,128]{1,0:T(8,128)} %bitcast.32), custom_call_target="tpu_custom_call" | custom-call | tf_op jit(solution)/shard_map/pallas_call | solution.py:357
  79.5 0.9 reshape.152
  80.5 0.2 fusion
  80.7 1.7 %copy-done.3 = bf16[4672,256]{1,0:T(8,128)(2,1)S(1)} copy-done((bf16[4672,256]{1,0:T(8,128)(2,1)S(1)}, bf16[4672,256]{1,0:T(8,128)(2,1)}, u32[]{:S(2)}) %copy-start.3) | copy-done | bytes 2392088
  82.4 1.7 %copy-done.5 = f32[4,576,256]{2,1,0:T(8,128)S(1)} copy-done((f32[4,576,256]{2,1,0:T(8,128)S(1)}, f32[4,576,256]{2,1,0:T(8,128)}, u32[]{:S(2)}) %copy-start.5) | copy-done | bytes 2359320
  84.1 17.2 %shard_map.91 = f32[4,2,128]{2,1,0:T(2,128)S(1)} custom-call(f32[8,128]{1,0:T(8,128)S(1)} %reshape.153.coeff_ref, f32[4,576,256]{2,1,0:T(8,128)S(1)} %copy-done.5, f32[45,32,128]{2,1,0:T(8,128)S(1)} %slice.95.basis_ref, f32[104,128]{1,0:T(8,128)S(1)} %copy-done.4, bf16[4672,256]{1,0:T(8,128)(2,1)S(1)} %copy-done.3), custom_call_target="tpu_custom_call" | custom-call | flops 20000000000 | bytes 8388608 | tf_op jit(solution)/shard_map/pallas_call | solution.py:470
  101.3 0.6 copy-done.2
  101.9 10.0 %shard_map.92 = f32[32,8,128]{2,1,0:T(8,128)} custom-call(f32[8,128]{1,0:T(8,128)} %bitcast.33), custom_call_target="tpu_custom_call" | custom-call | tf_op jit(solution)/shard_map/pallas_call | solution.py:357
  111.9 0.9 reshape.155
  112.8 0.2 fusion.4
  113.1 0.7 reshape.157
  113.7 0.7 reshape.156
  (29 shorter events, 0.8 us)
Async XLA Ops:
  3.1 0.6 copy-start.9
  16.8 1.6 %copy-start = (f32[2,4,16,4096]{3,2,1,0:T(8,128)S(1)}, f32[2,4,16,4096]{3,2,1,0:T(8,128)}, u32[]{:S(2)}) copy-start(f32[2,4,16,4096]{3,2,1,0:T(8,128)} %param.13) | copy-start | bytes 6291460
  21.6 5.0 %slice-start = ((f32[32,8,128]{2,1,0:T(8,128)}), f32[32,2,128]{2,1,0:T(2,128)S(1)}, s32[]{:S(2)}) async-start(f32[32,8,128]{2,1,0:T(8,128)} %shard_map.86), calls=%async_computation.1 | async-start | bytes 65536 | tf_op jit(solution)/shard_map/slice | solution.py:393
  21.6 31.1 %all-to-all-start = ((f32[32,128,128]{2,1,0:T(8,128)}), f32[32,128,128]{2,1,0:T(8,128)S(1)}, u32[]{:S(2)}, u32[]{:S(2)}) async-start(f32[32,128,128]{2,1,0:T(8,128)} %shard_map.87), calls=%async_computation | async-start | bytes 4194304 | tf_op jit(solution)/shard_map/all_to_all | solution.py:421
  26.1 2.1 %copy-start.4 = (f32[104,128]{1,0:T(8,128)S(1)}, f32[104,128]{1,0:T(8,128)}, u32[]{:S(2)}) copy-start(f32[104,128]{1,0:T(8,128)} %constant.128.clone.fixed_ref) | copy-start | bytes 159748
  37.2 1.5 %copy-start.6 = (f32[4,576,256]{2,1,0:T(8,128)}, f32[4,576,256]{2,1,0:T(8,128)S(1)}, u32[]{:S(2)}) copy-start(f32[4,576,256]{2,1,0:T(8,128)S(1)} %get-tuple-element.43.otf_ref) | copy-start | bytes 7077892
  38.7 1.0 copy-start.7
  52.7 1.2 %copy-start.8 = (f32[4,256,256]{2,1,0:T(8,128)S(1)}, f32[4,256,256]{2,1,0:T(8,128)}, u32[]{:S(2)}) copy-start(f32[4,256,256]{2,1,0:T(8,128)} %copy-done.7) | copy-start | bytes 3145732
  68.9 0.6 copy-start.1
  80.7 1.7 %copy-start.3 = (bf16[4672,256]{1,0:T(8,128)(2,1)S(1)}, bf16[4672,256]{1,0:T(8,128)(2,1)}, u32[]{:S(2)}) copy-start(bf16[4672,256]{1,0:T(8,128)(2,1)} %constant.127.clone.pack_ref) | copy-start | bytes 7176196
  82.4 1.7 %copy-start.5 = (f32[4,576,256]{2,1,0:T(8,128)S(1)}, f32[4,576,256]{2,1,0:T(8,128)}, u32[]{:S(2)}) copy-start(f32[4,576,256]{2,1,0:T(8,128)} %get-tuple-element.47.data_ref) | copy-start | bytes 7077892
  101.3 0.6 copy-start.2

commit v5 on v4

--- a/solution.py
+++ b/solution.py
@@ -315,41 +315,41 @@
 
 def gather_kernel(n, block_ref, out_ref, send_sem, recv_sem):
     me = lax.axis_index("sub")
+    group = n // TR
+    start = (me // group) * group
+    place = lax.rem(me, group)
+    inside = [start + lax.rem(place + step, group) for step in range(1, group)]
+    across = [lax.rem(me + step * group, n) for step in range(1, TR)]
     barrier = pltpu.get_barrier_semaphore()
-
-    def greet(step, carry):
-        pl.semaphore_signal(
-            barrier,
-            inc=1,
-            device_id=(lax.rem(me + step, n),),
-            device_id_type=pl.DeviceIdType.MESH,
-        )
-        return carry
-
-    lax.fori_loop(1, n, greet, 0)
-    pl.semaphore_wait(barrier, n - 1)
-
-    def copy_to(step):
-        return pltpu.make_async_remote_copy(
-            src_ref=block_ref,
-            dst_ref=out_ref.at[me],
-            send_sem=send_sem.at[step],
-            recv_sem=recv_sem.at[step],
-            device_id=(lax.rem(me + step, n),),
-            device_id_type=pl.DeviceIdType.MESH,
-        )
-
-    def begin(step, carry):
-        copy_to(step).start()
-        return carry
-
-    def finish(step, carry):
-        copy_to(step).wait()
-        return carry
-
-    lax.fori_loop(1, n, begin, 0)
+    for peer in inside + across:
+        pl.semaphore_signal(barrier, inc=1, device_id=(peer,), device_id_type=pl.DeviceIdType.MESH)
+    pl.semaphore_wait(barrier, len(inside) + len(across))
+
+    def copies(source, target, peers, first):
+        return [
+            pltpu.make_async_remote_copy(
+                src_ref=source,
+                dst_ref=target,
+                send_sem=send_sem.at[first + k],
+                recv_sem=recv_sem.at[first + k],
+                device_id=(peer,),
+                device_id_type=pl.DeviceIdType.MESH,
+            )
+            for k, peer in enumerate(peers)
+        ]
+
+    stage = copies(block_ref, out_ref.at[me], inside, 0)
+    for copy in stage:
+        copy.start()
     out_ref[me] = block_ref[...]
-    lax.fori_loop(1, n, finish, 0)
+    for copy in stage:
+        copy.wait()
+    team = out_ref.at[pl.ds(start, group)]
+    stage = copies(team, team, across, len(inside))
+    for copy in stage:
+        copy.start()
+    for copy in stage:
+        copy.wait()
 
 
 def spread_blocks(block, ident):

time: 115 us -> 121 us (1.052)
  Pallas kernels: 76.4 us -> 83 us
    pallas_call x3, Pallas kernels: 32 us -> 38.7 us  [spread_blocks(): pl.pallas_call(functools.partial(gather_kernel, n), out_shape=jax.ShapeDt...]
where the time goes in v5:
time: 121 us; the launch traced here: 120 us
  Pallas kernels  83 us (69%)
  local copies, waits for them, and re-layouts  16.6 us (14%)
  waiting for transfers between devices  13 us (11%)
  starting transfers between devices  3.73 us (3%)
  other arithmetic  2.55 us (2%)
    pallas_call x3, Pallas kernels, spread_blocks(): pl.pallas_call(functools.partial(gather_kernel, n), out_shape=jax.ShapeDt...  38.7 us
    pallas_call x1, Pallas kernels, later_slopes(): pl.pallas_call(functools.partial(joint_kernel, scale, modes, spots), grid...  17.2 us
    pallas_call x1, Pallas kernels, first_slopes(): pl.pallas_call(functools.partial(backward_kernel, scale, spots), grid=(pe...  14.9 us
    all_to_all x1, waiting for transfers between devices, on_device(): lax.all_to_all(windows, 'sub', 0, 0, axis_index_groups=teams, tiled=True)  13 us
    unnamed x21, local copies, waits for them, and re-layouts  11.7 us
    pallas_call x1, Pallas kernels, first_slopes(): pl.pallas_call(functools.partial(forward_kernel, scale, modes, spots), gr...  9.03 us
    all_to_all x1, starting transfers between devices, on_device(): lax.all_to_all(windows, 'sub', 0, 0, axis_index_groups=teams, tiled=True)  3.73 us
    pallas_call x1, Pallas kernels, on_device(): pl.pallas_call(functools.partial(window_kernel, batch), grid_spec=pltpu.P...  3.2 us
  transfers between devices with their start and end apart: 1, of which 1 were waited for; matrix products, arithmetic and copies ran while one was open for 2% of the time, Pallas kernels for 8%

profile of v5, /device:TPU:0, one launch (start us, length us, event | category | flops | bytes accessed | tf_op | source)
XLA Modules:
  0.0 120.3 jit_solution(15271843423604408154)
XLA Ops:
  0.7 0.7 convert_bitcast_fusion
  1.3 0.7 convert_bitcast_fusion.1
  2.0 0.7 pad.13
  2.9 0.2 scatter.14.block_ref
  3.1 0.6 copy-done.9
  3.7 14.8 %shard_map.86 = f32[32,8,128]{2,1,0:T(8,128)} custom-call(f32[8,128]{1,0:T(8,128)} %copy-done.9), custom_call_target="tpu_custom_call" | custom-call | tf_op jit(solution)/shard_map/pallas_call | solution.py:357
  18.5 1.0 fusion.14
  19.7 1.6 %copy-done = f32[2,4,16,4096]{3,2,1,0:T(8,128)S(1)} copy-done((f32[2,4,16,4096]{3,2,1,0:T(8,128)S(1)}, f32[2,4,16,4096]{3,2,1,0:T(8,128)}, u32[]{:S(2)}) %copy-start) | copy-done | bytes 2097176
  21.3 3.2 %shard_map.87 = f32[32,128,128]{2,1,0:T(8,128)} custom-call(s32[32]{0:T(128)S(1)} %convert_element_type.23.anchor_ref, f32[128,4096]{1,0:T(8,128)S(1)} %bitcast.30), custom_call_target="tpu_custom_call" | custom-call | tf_op jit(solution)/shard_map/pallas_call | solution.py:409
  24.5 3.7 %all-to-all-start = ((f32[32,128,128]{2,1,0:T(8,128)}), f32[32,128,128]{2,1,0:T(8,128)S(1)}, u32[]{:S(2)}, u32[]{:S(2)}) async-start(f32[32,128,128]{2,1,0:T(8,128)} %shard_map.87), calls=%async_computation | async-start | bytes 4194304 | tf_op jit(solution)/shard_map/all_to_all | solution.py:421
  28.4 0.2 dynamic-slice_reduce_fusion
  28.7 0.2 fusion.1
  28.9 1.3 %copy.14 = f32[6,8,32,128]{3,2,1,0:T(8,128)S(1)} copy(f32[6,8,32,128]{3,1,2,0:T(8,128)} %bitcast.35) | data formatting | bytes 1572864
  30.3 9.0 %shard_map.88 = (f32[4,576,256]{2,1,0:T(8,128)S(1)}, f32[4,256,1024]{2,1,0:T(8,128)}, f32[4,256,256]{2,1,0:T(8,128)S(1)}) custom-call(f32[8,128]{1,0:T(8,128)S(1)} %reshape.149.coeff_ref, f32[45,32,128]{2,1,0:T(8,128)S(1)} %slice.95.basis_ref, f32[104,128]{1,0:T(8,128)S(1)} %copy-done.4, bf16[4672,256]{1,0:T(8,128)(2,1)} %constant.127.clone.pack_ref), custom_call_target="tpu_custom_call" | custom-call | flops 10000000000 | bytes 8388608 | tf_op jit(solution)/shard_map/pallas_call | solution.py:445
  39.3 1.5 %copy-done.6 = f32[4,576,256]{2,1,0:T(8,128)} copy-done((f32[4,576,256]{2,1,0:T(8,128)}, f32[4,576,256]{2,1,0:T(8,128)S(1)}, u32[]{:S(2)}) %copy-start.6) | copy-done | bytes 2359320
  40.8 1.0 copy-done.7
  41.8 13.0 %all-to-all-done = f32[32,128,128]{2,1,0:T(8,128)S(1)} async-done(((f32[32,128,128]{2,1,0:T(8,128)}), f32[32,128,128]{2,1,0:T(8,128)S(1)}, u32[]{:S(2)}, u32[]{:S(2)}) %all-to-all-start) | async-done | bytes 2097184 | tf_op jit(solution)/shard_map/all_to_all | solution.py:421
  54.8 1.2 %copy-done.8 = f32[4,256,256]{2,1,0:T(8,128)S(1)} copy-done((f32[4,256,256]{2,1,0:T(8,128)S(1)}, f32[4,256,256]{2,1,0:T(8,128)}, u32[]{:S(2)}) %copy-start.8) | copy-done | bytes 1048600
  56.0 14.9 %shard_map.89 = (f32[4,576,256]{2,1,0:T(8,128)}, f32[4,2,128]{2,1,0:T(2,128)S(1)}) custom-call(f32[8,4,2,4,16,128]{5,4,3,2,1,0:T(8,128)S(1)} %bitcast.31, f32[4,576,256]{2,1,0:T(8,128)} %copy-done.6, f32[4,256,1024]{2,1,0:T(8,128)} %get-tuple-element.44.field_ref, f32[4,256,256]{2,1,0:T(8,128)S(1)} %copy-done.8, f32[45,32,128]{2,1,0:T(8,128)S(1)} %slice.95.basis_ref, ...), custom_call_target="tpu_custom_call" | custom-call | flops 10000000000 | bytes 8388608 | tf_op jit(solution)/shard_map/pallas_call | solution.py:457
  70.9 0.6 copy-done.1
  71.5 11.7 %shard_map.90 = f32[32,8,128]{2,1,0:T(8,128)} custom-call(f32[8,128]{1,0:T(8,128)} %bitcast.32), custom_call_target="tpu_custom_call" | custom-call | tf_op jit(solution)/shard_map/pallas_call | solution.py:357
  83.2 0.9 reshape.152
  84.2 0.2 fusion
  84.4 1.7 %copy-done.3 = bf16[4672,256]{1,0:T(8,128)(2,1)S(1)} copy-done((bf16[4672,256]{1,0:T(8,128)(2,1)S(1)}, bf16[4672,256]{1,0:T(8,128)(2,1)}, u32[]{:S(2)}) %copy-start.3) | copy-done | bytes 2392088
  86.1 1.7 %copy-done.5 = f32[4,576,256]{2,1,0:T(8,128)S(1)} copy-done((f32[4,576,256]{2,1,0:T(8,128)S(1)}, f32[4,576,256]{2,1,0:T(8,128)}, u32[]{:S(2)}) %copy-start.5) | copy-done | bytes 2359320
  87.7 17.2 %shard_map.91 = f32[4,2,128]{2,1,0:T(2,128)S(1)} custom-call(f32[8,128]{1,0:T(8,128)S(1)} %reshape.153.coeff_ref, f32[4,576,256]{2,1,0:T(8,128)S(1)} %copy-done.5, f32[45,32,128]{2,1,0:T(8,128)S(1)} %slice.95.basis_ref, f32[104,128]{1,0:T(8,128)S(1)} %copy-done.4, bf16[4672,256]{1,0:T(8,128)(2,1)S(1)} %copy-done.3), custom_call_target="tpu_custom_call" | custom-call | flops 20000000000 | bytes 8388608 | tf_op jit(solution)/shard_map/pallas_call | solution.py:470
  104.9 0.6 copy-done.2
  105.5 12.2 %shard_map.92 = f32[32,8,128]{2,1,0:T(8,128)} custom-call(f32[8,128]{1,0:T(8,128)} %bitcast.33), custom_call_target="tpu_custom_call" | custom-call | tf_op jit(solution)/shard_map/pallas_call | solution.py:357
  117.8 0.9 reshape.155
  118.7 0.2 fusion.4
  118.9 0.7 reshape.157
  119.6 0.7 reshape.156
  (29 shorter events, 0.8 us)
Async XLA Ops:
  3.1 0.6 copy-start.9
  19.7 1.6 %copy-start = (f32[2,4,16,4096]{3,2,1,0:T(8,128)S(1)}, f32[2,4,16,4096]{3,2,1,0:T(8,128)}, u32[]{:S(2)}) copy-start(f32[2,4,16,4096]{3,2,1,0:T(8,128)} %param.13) | copy-start | bytes 6291460
  24.5 4.3 %slice-start = ((f32[32,8,128]{2,1,0:T(8,128)}), f32[32,2,128]{2,1,0:T(2,128)S(1)}, s32[]{:S(2)}) async-start(f32[32,8,128]{2,1,0:T(8,128)} %shard_map.86), calls=%async_computation.1 | async-start | bytes 65536 | tf_op jit(solution)/shard_map/slice | solution.py:393
  24.5 30.3 %all-to-all-start = ((f32[32,128,128]{2,1,0:T(8,128)}), f32[32,128,128]{2,1,0:T(8,128)S(1)}, u32[]{:S(2)}, u32[]{:S(2)}) async-start(f32[32,128,128]{2,1,0:T(8,128)} %shard_map.87), calls=%async_computation | async-start | bytes 4194304 | tf_op jit(solution)/shard_map/all_to_all | solution.py:421
  28.2 2.1 %copy-start.4 = (f32[104,128]{1,0:T(8,128)S(1)}, f32[104,128]{1,0:T(8,128)}, u32[]{:S(2)}) copy-start(f32[104,128]{1,0:T(8,128)} %constant.128.clone.fixed_ref) | copy-start | bytes 159748
  39.3 1.5 %copy-start.6 = (f32[4,576,256]{2,1,0:T(8,128)}, f32[4,576,256]{2,1,0:T(8,128)S(1)}, u32[]{:S(2)}) copy-start(f32[4,576,256]{2,1,0:T(8,128)S(1)} %get-tuple-element.43.otf_ref) | copy-start | bytes 7077892
  40.8 1.0 copy-start.7
  54.8 1.2 %copy-start.8 = (f32[4,256,256]{2,1,0:T(8,128)S(1)}, f32[4,256,256]{2,1,0:T(8,128)}, u32[]{:S(2)}) copy-start(f32[4,256,256]{2,1,0:T(8,128)} %copy-done.7) | copy-start | bytes 3145732
  70.9 0.6 copy-start.1
  84.4 1.7 %copy-start.3 = (bf16[4672,256]{1,0:T(8,128)(2,1)S(1)}, bf16[4672,256]{1,0:T(8,128)(2,1)}, u32[]{:S(2)}) copy-start(bf16[4672,256]{1,0:T(8,128)(2,1)} %constant.127.clone.pack_ref) | copy-start | bytes 7176196
  86.1 1.7 %copy-start.5 = (f32[4,576,256]{2,1,0:T(8,128)S(1)}, f32[4,576,256]{2,1,0:T(8,128)}, u32[]{:S(2)}) copy-start(f32[4,576,256]{2,1,0:T(8,128)} %get-tuple-element.47.data_ref) | copy-start | bytes 7077892
  104.9 0.6 copy-start.2
